TPU v7x, 32 devices: a whole 2x2x4 slice. The times are simulated.
32 devices in a mesh: pipe: 4 (over y, x), expert: 8 (over z, core).
Axes of the slice: x: 2, y: 2, z: 4, core: 2. Of those that a mesh axis runs over, the one named last changes fastest.
Arguments:
- acts_a: bfloat16 [4, 512, 7168], P('pipe', 'expert'), may hold values from -6 to 6
- acts_b: bfloat16 [4, 512, 7168], P('pipe', 'expert'), may hold values from -6 to 6
- cot_b: bfloat16 [4, 512, 7168], P('pipe', 'expert'), may hold values from -1.5 to 1.5
- routes_a: int32 [4, 512, 2], P('pipe', 'expert'), may hold values from 0 to 3, all different within a row; in each aligned block of 64 rows (0 to 63, 64 to 127, ..., all dimensions but the last counted through in order) at most 34 rows name the same one
- gates_a: float32 [4, 512, 2], P('pipe', 'expert'), may hold values from 0.1 to 1
- routes_b: int32 [4, 512, 2], P('pipe', 'expert'), may hold values from 0 to 3, all different within a row; in each aligned block of 64 rows (0 to 63, 64 to 127, ..., all dimensions but the last counted through in order) at most 34 rows name the same one
- gates_b: float32 [4, 512, 2], P('pipe', 'expert'), may hold values from 0.1 to 1
- up_weight: bfloat16 [4, 28672, 1024], P('pipe', 'expert'), may hold values from -0.0625 to 0.0625
- down_weight: bfloat16 [4, 1024, 28672], P('pipe', None, 'expert'), may hold values from -0.1875 to 0.1875
- up_scale: float32 [4, 4], P('pipe'), may hold values from 0.002362278 to 0.004724556
- down_scale: float32 [4, 4], P('pipe'), may hold values from 0.00625 to 0.0125
Outputs:
- next_a: bfloat16 [4, 512, 7168], P('pipe', 'expert')
- next_cot_b: bfloat16 [4, 512, 7168], P('pipe', 'expert')
- up_grad: bfloat16 [4, 28672, 1024], P('pipe', 'expert')
- down_grad: bfloat16 [4, 1024, 28672], P('pipe', None, 'expert')
- up_scale_grad: float32 [4, 4], P('pipe')
- down_scale_grad: float32 [4, 4], P('pipe')
Inputs may be any that keep to these rules, and one draw needn't show every extreme that they name: `routes_a`: within the rows of one device no expert is chosen by more than 34 rows, and some expert is chosen by exactly 34 rows there. `routes_b`: within the rows of one device no expert is chosen by more than 34 rows, and some expert is chosen by exactly 34 rows there.
All inputs are finite; a program needn't handle non-finite values.
Results may differ from a plain program's by a relative error of at most 0.0091.
Values may be sent and summed in bfloat16 or wider, within the bound.
No kernel may reach another device: no remote copies, remote signals or barrier semaphores. Data moves between devices by JAX's collectives and lax.ppermute only.
A program may use at most 128 MiB of HBM per device.

v0:
```python
import math

import jax
import jax.numpy as jnp
from jax import lax
from jax.sharding import PartitionSpec as P

EXPERTS = 4
CAP = 34
CHUNKS = 4


qlimit = 7.0
epsilon = 1e-06

F_POLY = (3.99999827, -10.31875998, 10.67036777, -6.06749521, 1.94699036)
W_POLY = (19.73920584, -64.93916223, 85.45076959, -60.17190643, 25.98146098, -6.54589238)


def horner(coefs, z):
    acc = jnp.full_like(z, coefs[-1])
    for c in coefs[-2::-1]:
        acc = acc * z + c
    return acc


def reduced(weights, inv_scale):
    u = jnp.clip(weights.astype(jnp.float32) * inv_scale, -qlimit, qlimit)
    return u, u - jnp.round(u)


def fake_quant(weights, scale, inv_scale):
    u, r = reduced(weights, inv_scale)
    z = r * r
    return (scale * (u - r * ((0.25 - z) * horner(F_POLY, z)))).astype(jnp.bfloat16)


def quant_grads(weights, inv_scale, grads):
    u, r = reduced(weights, inv_scale)
    z = r * r
    weight_grad = grads * (z * horner(W_POLY, z))
    return weight_grad.astype(jnp.bfloat16), jnp.sum(weight_grad * u)


def dot(a, b, dims=(((1,), (0,)), ((), ()))):
    return lax.dot_general(a, b, dims, preferred_element_type=jnp.float32)


def rounded(value):
    return lax.reduce_precision(value, exponent_bits=8, mantissa_bits=7)


def after(value, *others):
    return lax.optimization_barrier((value, others))[0]


LAST = (((1,), (1,)), ((), ()))
FIRST = (((0,), (0,)), ((), ()))


def section(
    acts_a,
    acts_b,
    cot_b,
    routes_a,
    gates_a,
    routes_b,
    gates_b,
    up_weight,
    down_weight,
    up_scale,
    down_scale,
):
    peers = lax.axis_size("expert")
    stages = lax.axis_size("pipe")
    parts = peers // EXPERTS
    device_id = lax.axis_index("expert")
    expert_id = device_id // parts
    part_id = device_id % parts
    tokens, width = acts_a.shape[1], acts_a.shape[2]
    part_width = width // parts

    def swap(value, distance):
        return lax.ppermute(value, "expert", [(i, i ^ distance) for i in range(peers)])

    def part_sum(value):
        distance = 1
        while distance < parts:
            value = value + swap(value, distance)
            distance *= 2
        return value

    def token_sum(value):
        distance = 1
        while distance < parts:
            other = jnp.split(swap(value, distance), parts, axis=0)
            value = value + jnp.concatenate([other[k ^ distance] for k in range(parts)], axis=0)
            distance *= 2
        return value

    def spread(value):
        pieces = []
        for k in range(parts):
            start = (part_id ^ k) * part_width
            piece = lax.dynamic_slice_in_dim(value, start, part_width, axis=1)
            pieces.append(swap(piece, k) if k else piece)
        return jnp.concatenate(pieces, axis=0)

    def share(value):
        pieces = [swap(value, k) if k else value for k in range(parts)]
        return jnp.concatenate(pieces, axis=0)

    def exchange(blocks):
        return [swap(b, k * parts) if k else b for k, b in enumerate(blocks)]

    def pass_on(value, by):
        pieces = []
        for k in range(parts):
            block = value[k * tokens : (k + 1) * tokens]
            pairs = [
                (s * peers + i, (s + by) * peers + (i ^ k))
                for s in range(stages)
                if 0 <= s + by < stages
                for i in range(peers)
            ]
            pieces.append(lax.ppermute(block, ("pipe", "expert"), pairs))
        return pieces

    def in_columns(chunks):
        columns = []
        for q in range(parts):
            for pieces in chunks:
                column = pieces[0]
                for k in range(1, parts):
                    column = jnp.where((part_id ^ k) == q, pieces[k], column)
                columns.append(column)
        return jnp.concatenate(columns, axis=1)

    def one_hots(routes):
        near = jnp.bitwise_xor(routes, expert_id)
        matches = (near[:, :, None] == jnp.arange(EXPERTS)).astype(jnp.float32)
        both = matches.sum(1)
        lower = (jnp.arange(tokens)[:, None] > jnp.arange(tokens)[None, :]).astype(jnp.float32)
        earlier = dot(lower, both)
        chosen, seen = [], earlier
        for j in range(routes.shape[1]):
            m = matches[:, j]
            slot = jnp.sum(m * seen, axis=1)
            at_slot = (slot[:, None] == jnp.arange(CAP, dtype=jnp.float32)).astype(jnp.float32)
            chosen.append(m[:, :, None] * at_slot[:, None, :])
            seen = seen + m
        return chosen

    def group_hots(routes):
        hots = []
        for block in range(parts):
            hots.append(one_hots(routes[block * tokens : (block + 1) * tokens]))
        out = []
        for j in range(routes.shape[1]):
            rows = []
            for block in range(parts):
                here = (jnp.arange(parts) == (part_id ^ block)).astype(jnp.float32)
                rows.append(hots[block][j][:, :, None, :] * here[None, None, :, None])
            out.append(jnp.concatenate(rows, axis=0).reshape(parts * tokens, -1))
        return out

    def pack(hot, values):
        return dot(hot, values, FIRST)

    def split(rows):
        return jnp.split(rows, EXPERTS, axis=0)

    is_mine = (jnp.arange(EXPERTS, dtype=jnp.int32) == expert_id).astype(jnp.float32)
    s_up = jnp.sum(is_mine * up_scale[0])
    s_down = jnp.sum(is_mine * down_scale[0])
    inv_up, inv_down = 1.0 / s_up, 1.0 / s_down
    w_up, w_down = up_weight[0], down_weight[0]

    def inv_rms(x):
        wide = x.astype(jnp.float32)
        return lax.rsqrt(jnp.mean(wide * wide, axis=-1, keepdims=True) + epsilon)

    small = jnp.concatenate(
        [
            routes_b[0].astype(jnp.float32),
            gates_b[0],
            inv_rms(acts_b[0]),
            routes_a[0].astype(jnp.float32),
            gates_a[0],
            inv_rms(acts_a[0]),
        ],
        axis=1,
    )
    small = share(small)
    top = routes_a.shape[2]
    routes_gb, gates_gb, rms_b, routes_ga, gates_ga, rms_a = jnp.split(
        small, [top, 2 * top, 2 * top + 1, 3 * top + 1, 4 * top + 1], axis=1
    )
    x_b, c_b, x_a = spread(acts_b[0]), spread(cot_b[0]), spread(acts_a[0])

    hots_b = group_hots(routes_gb.astype(jnp.int32))
    hot_b = sum(hots_b).astype(jnp.bfloat16)
    gate_b = sum(jnp.sum(h * gates_gb[:, j : j + 1], axis=0) for j, h in enumerate(hots_b))
    norm_b = (x_b.astype(jnp.float32) * rms_b).astype(jnp.bfloat16)
    send_u = pack(hot_b, norm_b).astype(jnp.bfloat16)
    rows_u = jnp.concatenate(exchange(split(send_u)), axis=0)
    send_c = (pack(hot_b, after(c_b, send_u)) * gate_b[:, None]).astype(jnp.bfloat16)
    rows_c = jnp.concatenate(exchange(split(send_c)), axis=0)

    q_up = fake_quant(after(w_up, send_c), s_up, inv_up)
    q_down = fake_quant(after(w_down, q_up), s_down, inv_down)
    x_a = after(x_a, q_down)
    hots_a = [h.astype(jnp.bfloat16) for h in group_hots(routes_ga.astype(jnp.int32))]
    norm_a = (x_a.astype(jnp.float32) * rms_a).astype(jnp.bfloat16)
    send_a = pack(sum(hots_a), norm_a).astype(jnp.bfloat16)
    blocks_a = exchange(split(send_a))

    q_up, q_down = lax.optimization_barrier((q_up, q_down, send_a))[:2]

    own_pre_b = dot(rows_u, q_up)
    pre_b = rounded(part_sum(own_pre_b))
    own_grad = dot(rows_c, q_down, LAST)
    hidden_grad = rounded(part_sum(own_grad))
    sigma = jax.nn.sigmoid(pre_b)
    hidden_b = (pre_b * sigma).astype(jnp.bfloat16)
    pre_grad = (hidden_grad * sigma * (1.0 + pre_b * (1.0 - sigma))).astype(jnp.bfloat16)
    input_rows = dot(pre_grad, q_up, LAST).astype(jnp.bfloat16)
    back = jnp.concatenate(exchange(split(input_rows)), axis=0)

    rows_u, rows_c, own_pre_b, own_grad = lax.optimization_barrier(
        (rows_u, rows_c, own_pre_b, own_grad, input_rows)
    )[:4]
    dw_up, sum_up = quant_grads(w_up, inv_up, dot(rows_u, pre_grad, FIRST))
    dw_down, sum_down = quant_grads(w_down, inv_down, dot(hidden_b, rows_c, FIRST))
    quant_up = jnp.sum(pre_grad.astype(jnp.float32) * own_pre_b)
    quant_down = jnp.sum(hidden_b.astype(jnp.float32) * own_grad)
    root = math.sqrt(w_up.size * parts * qlimit)
    ds_up = (quant_up * inv_up - sum_up) / root
    ds_down = (quant_down * inv_down - sum_down) / root
    sums = jnp.stack([is_mine * ds_up, is_mine * ds_down])
    for c in range(peers.bit_length() - 1):
        sums = sums + swap(sums, 1 << c)

    rows_a = jnp.concatenate(after(blocks_a, dw_up, dw_down), axis=0)
    own_pre_a = dot(rows_a, q_up)
    pre_a = rounded(part_sum(own_pre_a))
    hidden_a = (pre_a * jax.nn.sigmoid(pre_a)).astype(jnp.bfloat16)
    pieces = CHUNKS
    step = part_width // pieces
    chunks = []
    for c in range(pieces):
        outputs = dot(hidden_a, q_down[:, c * step : (c + 1) * step]).astype(jnp.bfloat16)
        chunks.append(exchange(split(outputs)))

    grad = dot(hot_b, back)
    x_wide = x_b.astype(jnp.float32)
    own_inner = jnp.sum(x_wide * grad, axis=1, keepdims=True)
    inner = token_sum(own_inner)
    pull = rms_b * rms_b * rms_b * inner / width
    grad_in = c_b.astype(jnp.float32) + (rms_b * grad - x_wide * pull)
    next_cot = in_columns([pass_on(grad_in.astype(jnp.bfloat16), -1)])

    passed = []
    for c in range(pieces):
        done_a = jnp.concatenate(chunks[c], axis=0)
        mixed = x_a[:, c * step : (c + 1) * step].astype(jnp.float32)
        for j, h in enumerate(hots_a):
            mixed = mixed + gates_ga[:, j : j + 1] * dot(h, done_a)
        passed.append(pass_on(mixed.astype(jnp.bfloat16), 1))
    next_a = in_columns(passed)
    return (
        next_a[None],
        next_cot[None],
        dw_up[None],
        dw_down[None],
        sums[0][None],
        sums[1][None],
    )


def solution(mesh):
    tokens = P("pipe", "expert", None)
    columns = P("pipe", None, "expert")
    steps = P("pipe", None)
    return jax.shard_map(
        section,
        mesh=mesh,
        in_specs=(tokens,) * 8 + (columns, steps, steps),
        out_specs=(tokens, tokens, tokens, columns, steps, steps),
        check_vma=False,
    )
```

profile of v0, /device:TPU:0, one launch (start us, length us, event | category | flops | bytes accessed | tf_op | source)
XLA Modules:
  0.0 319.5 jit_solution(14867194892701558318)
XLA Ops:
  18.3 5.1 %collective-permute-start.12 = (bf16[68,3584]{1,0:T(8,128)(2,1)S(1)}, bf16[68,3584]{1,0:T(8,128)(2,1)S(1)}, u32[]{:S(2)}, u32[]{:S(2)}) collective-permute-start(bf16[68,3584]{1,0:T(8,128)(2,1)S(1)} %get-tuple-element.53), channel_id=1, source_target_pairs={{0,6},{1,7},{2,4},{3,5},{4,2},{5,3},{6,0},{7,1},{8,14},{9,15},{10,... | collective-permute-start | bytes 1462280 | tf_op jit(solution)/shard_map/ppermute | solution.py:84
  24.0 3.7 %collective-permute-start.9 = (bf16[68,3584]{1,0:T(8,128)(2,1)S(1)}, bf16[68,3584]{1,0:T(8,128)(2,1)S(1)}, u32[]{:S(2)}, u32[]{:S(2)}) collective-permute-start(bf16[68,3584]{1,0:T(8,128)(2,1)S(1)} %get-tuple-element.57), channel_id=1, source_target_pairs={{0,6},{1,7},{2,4},{3,5},{4,2},{5,3},{6,0},{7,1},{8,14},{9,15},{10,... | collective-permute-start | bytes 1462280 | tf_op jit(solution)/shard_map/ppermute | solution.py:84
  27.8 10.1 %multiply_convert_fusion.1 = bf16[3584,1024]{1,0:T(8,128)(2,1)S(1)} fusion(bf16[3584,1024]{1,0:T(8,128)(2,1)S(1)} %bitcast.141, f32[]{:T(128)S(6)} %div.43, f32[]{:T(128)} %fusion.95), kind=kLoop, calls=%fused_computation.18 | loop fusion | flops 73400320 | bytes 14680072 | tf_op jit(solution)/shard_map/convert_element_type | solution.py:35
  37.9 10.4 %multiply_convert_fusion = bf16[1024,3584]{1,0:T(8,128)(2,1)S(1)} fusion(bf16[1024,3584]{1,0:T(8,128)(2,1)S(1)} %bitcast.146, f32[]{:T(128)S(6)} %div.44, f32[]{:T(128)} %fusion.94), kind=kLoop, calls=%fused_computation.12 | loop fusion | flops 73400320 | bytes 14680072 | tf_op jit(solution)/shard_map/convert_element_type | solution.py:35
  50.6 8.0 %collective-permute-start.7 = (bf16[68,3584]{1,0:T(8,128)(2,1)S(1)}, bf16[68,3584]{1,0:T(8,128)(2,1)S(1)}, u32[]{:S(2)}, u32[]{:S(2)}) collective-permute-start(bf16[68,3584]{1,0:T(8,128)(2,1)S(1)} %get-tuple-element.59), channel_id=1, source_target_pairs={{0,2},{1,3},{2,0},{3,1},{4,6},{5,7},{6,4},{7,5},{8,10},{9,11},{10,... | collective-permute-start | bytes 1462280 | tf_op jit(solution)/shard_map/ppermute | solution.py:84
  58.7 32.1 %collective-permute-done.11 = bf16[68,3584]{1,0:T(8,128)(2,1)S(1)} collective-permute-done((bf16[68,3584]{1,0:T(8,128)(2,1)S(1)}, bf16[68,3584]{1,0:T(8,128)(2,1)S(1)}, u32[]{:S(2)}, u32[]{:S(2)}) %collective-permute-start.11) | collective-permute-done | bytes 487456 | tf_op jit(solution)/shard_map/ppermute | solution.py:84
  91.0 3.2 %fusion.129 = f32[272,1024]{1,0:T(8,128)} fusion(bf16[272,3584]{1,0:T(8,128)(2,1)S(1)} %pad_maximum_fusion.1, bf16[1024,3584]{1,0:T(8,128)(2,1)S(1)} %multiply_convert_fusion), kind=kOutput, calls=%fused_computation.274 | convolution fusion | flops 1996488704 | bytes 10403840 | tf_op jit(solution)/shard_map/dot_general | solution.py:46
  94.3 17.7 %collective-permute-done.8 = bf16[68,3584]{1,0:T(8,128)(2,1)S(1)} collective-permute-done((bf16[68,3584]{1,0:T(8,128)(2,1)S(1)}, bf16[68,3584]{1,0:T(8,128)(2,1)S(1)}, u32[]{:S(2)}, u32[]{:S(2)}) %collective-permute-start.8) | collective-permute-done | bytes 487456 | tf_op jit(solution)/shard_map/ppermute | solution.py:84
  129.3 15.1 %multiply_reduce_fusion.1 = (f32[]{:T(128)}, bf16[3584,1024]{1,0:T(8,128)(2,1)}) fusion(f32[]{:T(128)S(6)} %div.43, bf16[1,3584,1024]{2,1,0:T(8,128)(2,1)S(1)} %bitcast.143, bf16[272,3584]{1,0:T(8,128)(2,1)S(1)} %copy-done.12, bf16[272,1024]{1,0:T(8,128)(2,1)S(1)} %multiply_convert_fusion.5), kind=kOutput, calls=%fused_computation.7 | convolution fusion | flops 2073559040 | bytes 17186824 | tf_op jit(solution)/shard_map/dot_general | solution.py:46
  144.4 2.7 multiply_reduce_fusion.4
  147.1 14.6 %multiply_reduce_fusion = (f32[]{:T(128)}, bf16[1024,3584]{1,0:T(8,128)(2,1)}) fusion(f32[]{:T(128)S(6)} %div.44, bf16[1,1024,3584]{2,1,0:T(8,128)(2,1)S(1)} %bitcast.148, bf16[272,1024]{1,0:T(8,128)(2,1)S(1)} %get-tuple-element.43, bf16[272,3584]{1,0:T(8,128)(2,1)S(1)} %copy-done.10), kind=kOutput, calls=%fused_computation.6 | convolution fusion | flops 2073559040 | bytes 17186824 | tf_op jit(solution)/shard_map/dot_general | solution.py:46
  167.2 18.2 %collective-permute-done.5 = bf16[68,3584]{1,0:T(8,128)(2,1)} collective-permute-done((bf16[68,3584]{1,0:T(8,128)(2,1)}, bf16[68,3584]{1,0:T(8,128)(2,1)}, u32[]{:S(2)}, u32[]{:S(2)}) %collective-permute-start.5) | collective-permute-done | bytes 487456 | tf_op jit(solution)/shard_map/ppermute | solution.py:84
  185.5 21.5 %collective-permute-done.37 = bf16[68,3584]{1,0:T(8,128)(2,1)} collective-permute-done((bf16[68,3584]{1,0:T(8,128)(2,1)}, bf16[68,3584]{1,0:T(8,128)(2,1)}, u32[]{:S(2)}, u32[]{:S(2)}) %collective-permute-start.37) | collective-permute-done | bytes 487456 | tf_op jit(solution)/shard_map/ppermute | solution.py:84
  209.4 5.9 %fusion.7 = f32[272,1024]{1,0:T(8,128)S(1)} fusion(bf16[3584,1024]{1,0:T(8,128)(2,1)} %copy-done.1, bf16[68,3584]{1,0:T(8,128)(2,1)} %collective-permute-done.6, bf16[68,3584]{1,0:T(8,128)(2,1)} %collective-permute-done.5, bf16[68,3584]{1,0:T(8,128)(2,1)} %collective-permute-done.4, bf16[68,3584]{1,0:T(8,128)(2,1)S(1)} %copy-done.24), kind=kOutput, calls=%fused_computation.34 | convolution fusion | flops 2004287488 | bytes 10403840 | tf_op jit(solution)/shard_map/dot_general | solution.py:46
  219.6 3.6 %collective-permute-done.43 = f32[2,4]{1,0:T(2,128)S(1)} collective-permute-done((f32[2,4]{1,0:T(2,128)S(1)}, f32[2,4]{1,0:T(2,128)S(1)}, u32[]{:S(2)}, u32[]{:S(2)}) %collective-permute-start.43) | collective-permute-done | bytes 64 | tf_op jit(solution)/shard_map/ppermute | solution.py:84
  223.3 4.5 %collective-permute-done.44 = f32[2,4]{1,0:T(2,128)S(1)} collective-permute-done((f32[2,4]{1,0:T(2,128)S(1)}, f32[2,4]{1,0:T(2,128)S(1)}, u32[]{:S(2)}, u32[]{:S(2)}) %collective-permute-start.44) | collective-permute-done | bytes 64 | tf_op jit(solution)/shard_map/ppermute | solution.py:84
  228.3 3.9 %collective-permute-done.41 = bf16[64,3584]{1,0:T(8,128)(2,1)S(1)} collective-permute-done((bf16[64,3584]{1,0:T(8,128)(2,1)S(1)}, bf16[64,3584]{1,0:T(8,128)(2,1)S(1)}, u32[]{:S(2)}, u32[]{:S(2)}) %collective-permute-start.41) | collective-permute-done | bytes 458784 | tf_op jit(solution)/shard_map/ppermute | solution.py:126
  232.2 7.9 %collective-permute-done.40 = bf16[64,3584]{1,0:T(8,128)(2,1)S(1)} collective-permute-done((bf16[64,3584]{1,0:T(8,128)(2,1)S(1)}, bf16[64,3584]{1,0:T(8,128)(2,1)S(1)}, u32[]{:S(2)}, u32[]{:S(2)}) %collective-permute-start.40) | collective-permute-done | bytes 458784 | tf_op jit(solution)/shard_map/ppermute | solution.py:126
  246.1 3.1 collective-permute-start.31
  254.0 4.7 %collective-permute-done.32 = bf16[68,896]{1,0:T(8,128)(2,1)S(1)} collective-permute-done((bf16[68,896]{1,0:T(8,128)(2,1)S(1)}, bf16[68,896]{1,0:T(8,128)(2,1)S(1)}, u32[]{:S(2)}, u32[]{:S(2)}) %collective-permute-start.32) | collective-permute-done | bytes 121888 | tf_op jit(solution)/shard_map/ppermute | solution.py:84
  263.3 14.5 %collective-permute-done.27 = bf16[68,896]{1,0:T(8,128)(2,1)S(1)} collective-permute-done((bf16[68,896]{1,0:T(8,128)(2,1)S(1)}, bf16[68,896]{1,0:T(8,128)(2,1)S(1)}, u32[]{:S(2)}, u32[]{:S(2)}) %collective-permute-start.27) | collective-permute-done | bytes 121888 | tf_op jit(solution)/shard_map/ppermute | solution.py:84
  280.4 9.0 %collective-permute-start.21 = (bf16[68,896]{1,0:T(8,128)(2,1)S(1)}, bf16[68,896]{1,0:T(8,128)(2,1)S(1)}, u32[]{:S(2)}, u32[]{:S(2)}) collective-permute-start(bf16[68,896]{1,0:T(8,128)(2,1)S(1)} %get-tuple-element.85), channel_id=1, source_target_pairs={{0,2},{1,3},{2,0},{3,1},{4,6},{5,7},{6,4},{7,5},{8,10},{9,11},{10,... | collective-permute-start | bytes 365576 | tf_op jit(solution)/shard_map/ppermute | solution.py:84
  291.7 4.3 %collective-permute-start.35 = (bf16[64,896]{1,0:T(8,128)(2,1)S(1)}, bf16[64,896]{1,0:T(8,128)(2,1)S(1)}, u32[]{:S(2)}, u32[]{:S(2)}) collective-permute-start(bf16[64,896]{1,0:T(8,128)(2,1)S(1)} %get-tuple-element.93), channel_id=1, source_target_pairs={{0,8},{1,9},{2,10},{3,11},{4,12},{5,13},{6,14},{7,15},{8,16},{9,17... | collective-permute-start | bytes 344072 | tf_op jit(solution)/shard_map/ppermute | solution.py:126
  306.7 4.4 %collective-permute-start.25 = (bf16[64,896]{1,0:T(8,128)(2,1)S(1)}, bf16[64,896]{1,0:T(8,128)(2,1)S(1)}, u32[]{:S(2)}, u32[]{:S(2)}) collective-permute-start(bf16[64,896]{1,0:T(8,128)(2,1)S(1)} %get-tuple-element.97), channel_id=1, source_target_pairs={{0,8},{1,9},{2,10},{3,11},{4,12},{5,13},{6,14},{7,15},{8,16},{9,17... | collective-permute-start | bytes 344072 | tf_op jit(solution)/shard_map/ppermute | solution.py:126
  (287 shorter events, 85.4 us)
Async XLA Ops:
  9.5 38.8 %collective-permute-start = (bf16[64,3584]{1,0:T(8,128)(2,1)}, bf16[64,3584]{1,0:T(8,128)(2,1)}, u32[]{:S(2)}, u32[]{:S(2)}) collective-permute-start(bf16[64,3584]{1,0:T(8,128)(2,1)} %get-tuple-element.69), channel_id=1, source_target_pairs={{0,1},{1,0},{2,3},{3,2},{4,5},{5,4},{6,7},{7,6},{8,9},{9,8},{10,11... | collective-permute-start | bytes 1376264 | tf_op jit(solution)/shard_map/ppermute | solution.py:84
  18.3 32.3 %collective-permute-start.12 = (bf16[68,3584]{1,0:T(8,128)(2,1)S(1)}, bf16[68,3584]{1,0:T(8,128)(2,1)S(1)}, u32[]{:S(2)}, u32[]{:S(2)}) collective-permute-start(bf16[68,3584]{1,0:T(8,128)(2,1)S(1)} %get-tuple-element.53), channel_id=1, source_target_pairs={{0,6},{1,7},{2,4},{3,5},{4,2},{5,3},{6,0},{7,1},{8,14},{9,15},{10,... | collective-permute-start | bytes 1462280 | tf_op jit(solution)/shard_map/ppermute | solution.py:84
  23.4 67.3 %collective-permute-start.11 = (bf16[68,3584]{1,0:T(8,128)(2,1)S(1)}, bf16[68,3584]{1,0:T(8,128)(2,1)S(1)}, u32[]{:S(2)}, u32[]{:S(2)}) collective-permute-start(bf16[68,3584]{1,0:T(8,128)(2,1)S(1)} %get-tuple-element.54), channel_id=1, source_target_pairs={{0,4},{1,5},{2,6},{3,7},{4,0},{5,1},{6,2},{7,3},{8,12},{9,13},{10,... | collective-permute-start | bytes 1462280 | tf_op jit(solution)/shard_map/ppermute | solution.py:84
  23.4 67.3 %collective-permute-start.10 = (bf16[68,3584]{1,0:T(8,128)(2,1)S(1)}, bf16[68,3584]{1,0:T(8,128)(2,1)S(1)}, u32[]{:S(2)}, u32[]{:S(2)}) collective-permute-start(bf16[68,3584]{1,0:T(8,128)(2,1)S(1)} %get-tuple-element.55), channel_id=1, source_target_pairs={{0,2},{1,3},{2,0},{3,1},{4,6},{5,7},{6,4},{7,5},{8,10},{9,11},{10,... | collective-permute-start | bytes 1462280 | tf_op jit(solution)/shard_map/ppermute | solution.py:84
  24.0 70.2 %collective-permute-start.9 = (bf16[68,3584]{1,0:T(8,128)(2,1)S(1)}, bf16[68,3584]{1,0:T(8,128)(2,1)S(1)}, u32[]{:S(2)}, u32[]{:S(2)}) collective-permute-start(bf16[68,3584]{1,0:T(8,128)(2,1)S(1)} %get-tuple-element.57), channel_id=1, source_target_pairs={{0,6},{1,7},{2,4},{3,5},{4,2},{5,3},{6,0},{7,1},{8,14},{9,15},{10,... | collective-permute-start | bytes 1462280 | tf_op jit(solution)/shard_map/ppermute | solution.py:84
  48.3 63.6 %collective-permute-start.8 = (bf16[68,3584]{1,0:T(8,128)(2,1)S(1)}, bf16[68,3584]{1,0:T(8,128)(2,1)S(1)}, u32[]{:S(2)}, u32[]{:S(2)}) collective-permute-start(bf16[68,3584]{1,0:T(8,128)(2,1)S(1)} %get-tuple-element.58), channel_id=1, source_target_pairs={{0,4},{1,5},{2,6},{3,7},{4,0},{5,1},{6,2},{7,3},{8,12},{9,13},{10,... | collective-permute-start | bytes 1462280 | tf_op jit(solution)/shard_map/ppermute | solution.py:84
  50.6 61.3 %collective-permute-start.7 = (bf16[68,3584]{1,0:T(8,128)(2,1)S(1)}, bf16[68,3584]{1,0:T(8,128)(2,1)S(1)}, u32[]{:S(2)}, u32[]{:S(2)}) collective-permute-start(bf16[68,3584]{1,0:T(8,128)(2,1)S(1)} %get-tuple-element.59), channel_id=1, source_target_pairs={{0,2},{1,3},{2,0},{3,1},{4,6},{5,7},{6,4},{7,5},{8,10},{9,11},{10,... | collective-permute-start | bytes 1462280 | tf_op jit(solution)/shard_map/ppermute | solution.py:84
  94.2 26.1 %collective-permute-start.13 = (f32[272,1024]{1,0:T(8,128)}, f32[272,1024]{1,0:T(8,128)}, u32[]{:S(2)}, u32[]{:S(2)}) collective-permute-start(f32[272,1024]{1,0:T(8,128)} %fusion.129), channel_id=1, source_target_pairs={{0,1},{1,0},{2,3},{3,2},{4,5},{5,4},{6,7},{7,6},{8,9},{9,8},{10,11... | collective-permute-start | bytes 3342344 | tf_op jit(solution)/shard_map/ppermute | solution.py:84
  116.0 46.4 %collective-permute-start.6 = (bf16[68,3584]{1,0:T(8,128)(2,1)}, bf16[68,3584]{1,0:T(8,128)(2,1)}, u32[]{:S(2)}, u32[]{:S(2)}) collective-permute-start(bf16[68,3584]{1,0:T(8,128)(2,1)} %get-tuple-element.60), channel_id=1, source_target_pairs={{0,6},{1,7},{2,4},{3,5},{4,2},{5,3},{6,0},{7,1},{8,14},{9,15},{10,... | collective-permute-start | bytes 1462280 | tf_op jit(solution)/shard_map/ppermute | solution.py:84
  118.5 66.9 %collective-permute-start.5 = (bf16[68,3584]{1,0:T(8,128)(2,1)}, bf16[68,3584]{1,0:T(8,128)(2,1)}, u32[]{:S(2)}, u32[]{:S(2)}) collective-permute-start(bf16[68,3584]{1,0:T(8,128)(2,1)} %get-tuple-element.61), channel_id=1, source_target_pairs={{0,4},{1,5},{2,6},{3,7},{4,0},{5,1},{6,2},{7,3},{8,12},{9,13},{10,... | collective-permute-start | bytes 1462280 | tf_op jit(solution)/shard_map/ppermute | solution.py:84
  118.5 66.9 %collective-permute-start.4 = (bf16[68,3584]{1,0:T(8,128)(2,1)}, bf16[68,3584]{1,0:T(8,128)(2,1)}, u32[]{:S(2)}, u32[]{:S(2)}) collective-permute-start(bf16[68,3584]{1,0:T(8,128)(2,1)} %get-tuple-element.62), channel_id=1, source_target_pairs={{0,2},{1,3},{2,0},{3,1},{4,6},{5,7},{6,4},{7,5},{8,10},{9,11},{10,... | collective-permute-start | bytes 1462280 | tf_op jit(solution)/shard_map/ppermute | solution.py:84
  126.8 58.7 %collective-permute-start.38 = (bf16[68,3584]{1,0:T(8,128)(2,1)}, bf16[68,3584]{1,0:T(8,128)(2,1)}, u32[]{:S(2)}, u32[]{:S(2)}) collective-permute-start(bf16[68,3584]{1,0:T(8,128)(2,1)} %get-tuple-element.49), channel_id=1, source_target_pairs={{0,6},{1,7},{2,4},{3,5},{4,2},{5,3},{6,0},{7,1},{8,14},{9,15},{10,... | collective-permute-start | bytes 1462280 | tf_op jit(solution)/shard_map/ppermute | solution.py:84
  129.3 77.7 %collective-permute-start.37 = (bf16[68,3584]{1,0:T(8,128)(2,1)}, bf16[68,3584]{1,0:T(8,128)(2,1)}, u32[]{:S(2)}, u32[]{:S(2)}) collective-permute-start(bf16[68,3584]{1,0:T(8,128)(2,1)} %get-tuple-element.50), channel_id=1, source_target_pairs={{0,4},{1,5},{2,6},{3,7},{4,0},{5,1},{6,2},{7,3},{8,12},{9,13},{10,... | collective-permute-start | bytes 1462280 | tf_op jit(solution)/shard_map/ppermute | solution.py:84
  162.4 44.6 %collective-permute-start.36 = (bf16[68,3584]{1,0:T(8,128)(2,1)}, bf16[68,3584]{1,0:T(8,128)(2,1)}, u32[]{:S(2)}, u32[]{:S(2)}) collective-permute-start(bf16[68,3584]{1,0:T(8,128)(2,1)} %get-tuple-element.51), channel_id=1, source_target_pairs={{0,2},{1,3},{2,0},{3,1},{4,6},{5,7},{6,4},{7,5},{8,10},{9,11},{10,... | collective-permute-start | bytes 1462280 | tf_op jit(solution)/shard_map/ppermute | solution.py:84
  185.4 34.2 %collective-permute-start.42 = (f32[2,4]{1,0:T(2,128)S(1)}, f32[2,4]{1,0:T(2,128)S(1)}, u32[]{:S(2)}, u32[]{:S(2)}) collective-permute-start(f32[2,4]{1,0:T(2,128)S(1)} %pad_maximum_fusion.22), channel_id=1, source_target_pairs={{0,1},{1,0},{2,3},{3,2},{4,5},{5,4},{6,7},{7,6},{8,9},{9,8},{10,11... | collective-permute-start | bytes 104 | tf_op jit(solution)/shard_map/ppermute | solution.py:84
  215.3 25.9 %collective-permute-start.15 = (f32[272,1024]{1,0:T(8,128)S(1)}, f32[272,1024]{1,0:T(8,128)S(1)}, u32[]{:S(2)}, u32[]{:S(2)}) collective-permute-start(f32[272,1024]{1,0:T(8,128)S(1)} %fusion.7), channel_id=1, source_target_pairs={{0,1},{1,0},{2,3},{3,2},{4,5},{5,4},{6,7},{7,6},{8,9},{9,8},{10,11... | collective-permute-start | bytes 3342344 | tf_op jit(solution)/shard_map/ppermute | solution.py:84
  218.2 21.9 %collective-permute-start.40 = (bf16[64,3584]{1,0:T(8,128)(2,1)S(1)}, bf16[64,3584]{1,0:T(8,128)(2,1)S(1)}, u32[]{:S(2)}, u32[]{:S(2)}) collective-permute-start(bf16[64,3584]{1,0:T(8,128)(2,1)S(1)} %get-tuple-element.67), channel_id=1, source_target_pairs={{8,1},{9,0},{10,3},{11,2},{12,5},{13,4},{14,7},{15,6},{16,9},{17,8... | collective-permute-start | bytes 1376264 | tf_op jit(solution)/shard_map/ppermute | solution.py:126
  250.7 27.1 %collective-permute-start.27 = (bf16[68,896]{1,0:T(8,128)(2,1)S(1)}, bf16[68,896]{1,0:T(8,128)(2,1)S(1)}, u32[]{:S(2)}, u32[]{:S(2)}) collective-permute-start(bf16[68,896]{1,0:T(8,128)(2,1)S(1)} %get-tuple-element.80), channel_id=1, source_target_pairs={{0,4},{1,5},{2,6},{3,7},{4,0},{5,1},{6,2},{7,3},{8,12},{9,13},{10,... | collective-permute-start | bytes 365576 | tf_op jit(solution)/shard_map/ppermute | solution.py:84
  253.1 24.7 %collective-permute-start.26 = (bf16[68,896]{1,0:T(8,128)(2,1)S(1)}, bf16[68,896]{1,0:T(8,128)(2,1)S(1)}, u32[]{:S(2)}, u32[]{:S(2)}) collective-permute-start(bf16[68,896]{1,0:T(8,128)(2,1)S(1)} %get-tuple-element.81), channel_id=1, source_target_pairs={{0,2},{1,3},{2,0},{3,1},{4,6},{5,7},{6,4},{7,5},{8,10},{9,11},{10,... | collective-permute-start | bytes 365576 | tf_op jit(solution)/shard_map/ppermute | solution.py:84
  258.6 39.8 %collective-permute-start.23 = (bf16[68,896]{1,0:T(8,128)(2,1)S(1)}, bf16[68,896]{1,0:T(8,128)(2,1)S(1)}, u32[]{:S(2)}, u32[]{:S(2)}) collective-permute-start(bf16[68,896]{1,0:T(8,128)(2,1)S(1)} %get-tuple-element.83), channel_id=1, source_target_pairs={{0,6},{1,7},{2,4},{3,5},{4,2},{5,3},{6,0},{7,1},{8,14},{9,15},{10,... | collective-permute-start | bytes 365576 | tf_op jit(solution)/shard_map/ppermute | solution.py:84
  260.0 41.1 %collective-permute-start.22 = (bf16[68,896]{1,0:T(8,128)(2,1)S(1)}, bf16[68,896]{1,0:T(8,128)(2,1)S(1)}, u32[]{:S(2)}, u32[]{:S(2)}) collective-permute-start(bf16[68,896]{1,0:T(8,128)(2,1)S(1)} %get-tuple-element.84), channel_id=1, source_target_pairs={{0,4},{1,5},{2,6},{3,7},{4,0},{5,1},{6,2},{7,3},{8,12},{9,13},{10,... | collective-permute-start | bytes 365576 | tf_op jit(solution)/shard_map/ppermute | solution.py:84
  280.4 22.6 %collective-permute-start.21 = (bf16[68,896]{1,0:T(8,128)(2,1)S(1)}, bf16[68,896]{1,0:T(8,128)(2,1)S(1)}, u32[]{:S(2)}, u32[]{:S(2)}) collective-permute-start(bf16[68,896]{1,0:T(8,128)(2,1)S(1)} %get-tuple-element.85), channel_id=1, source_target_pairs={{0,2},{1,3},{2,0},{3,1},{4,6},{5,7},{6,4},{7,5},{8,10},{9,11},{10,... | collective-permute-start | bytes 365576 | tf_op jit(solution)/shard_map/ppermute | solution.py:84
  291.7 26.7 %collective-permute-start.35 = (bf16[64,896]{1,0:T(8,128)(2,1)S(1)}, bf16[64,896]{1,0:T(8,128)(2,1)S(1)}, u32[]{:S(2)}, u32[]{:S(2)}) collective-permute-start(bf16[64,896]{1,0:T(8,128)(2,1)S(1)} %get-tuple-element.93), channel_id=1, source_target_pairs={{0,8},{1,9},{2,10},{3,11},{4,12},{5,13},{6,14},{7,15},{8,16},{9,17... | collective-permute-start | bytes 344072 | tf_op jit(solution)/shard_map/ppermute | solution.py:126
  296.0 22.4 %collective-permute-start.34 = (bf16[64,896]{1,0:T(8,128)(2,1)S(1)}, bf16[64,896]{1,0:T(8,128)(2,1)S(1)}, u32[]{:S(2)}, u32[]{:S(2)}) collective-permute-start(bf16[64,896]{1,0:T(8,128)(2,1)S(1)} %get-tuple-element.94), channel_id=1, source_target_pairs={{0,9},{1,8},{2,11},{3,10},{4,13},{5,12},{6,15},{7,14},{8,17},{9,16... | collective-permute-start | bytes 344072 | tf_op jit(solution)/shard_map/ppermute | solution.py:126
  (59 other events, 866.3 us)
where the time goes:
time: 322 us; the launch traced here: 320 us
  waiting for transfers between devices  138 us (43%)
  starting transfers between devices  72.9 us (23%)
  matrix products  53.9 us (17%)
  other arithmetic  37.3 us (12%)
  local copies, waits for them, and re-layouts  11.3 us (4%)
  between operations  6.11 us (2%)
    ppermute x35, waiting for transfers between devices, swap(): lax.ppermute(value, 'expert', [(i, i ^ distance) for i in range(peers)])  122 us
    dot_general x26, matrix products, dot(): return lax.dot_general(a, b, dims, preferred_element_type=jnp.float32)  53.9 us
    ppermute x35, starting transfers between devices, swap(): lax.ppermute(value, 'expert', [(i, i ^ distance) for i in range(peers)])  49.7 us
    ppermute x10, starting transfers between devices, pass_on(): pieces.append(lax.ppermute(block, ('pipe', 'expert'), pairs))  23.2 us
    convert_element_type x2, other arithmetic, fake_quant(): (scale * (u - r * ((0.25 - z) * horner(F_POLY, z)))).astype(jnp.bfloat16)  20.4 us
    ppermute x10, waiting for transfers between devices, pass_on(): pieces.append(lax.ppermute(block, ('pipe', 'expert'), pairs))  16.3 us
  transfers between devices with their start and end apart: 45, of which 16 were waited for; matrix products, arithmetic and copies ran while one was open for 29% of the time, Pallas kernels for 0%

commit v1 on v0

--- a/solution.py
+++ b/solution.py
@@ -7,7 +7,7 @@
 
 EXPERTS = 4
 CAP = 34
-CHUNKS = 4
+CHUNKS = 3
 
 
 qlimit = 7.0
@@ -32,14 +32,14 @@
 def fake_quant(weights, scale, inv_scale):
     u, r = reduced(weights, inv_scale)
     z = r * r
-    return (scale * (u - r * ((0.25 - z) * horner(F_POLY, z)))).astype(jnp.bfloat16)
-
-
-def quant_grads(weights, inv_scale, grads):
-    u, r = reduced(weights, inv_scale)
-    z = r * r
-    weight_grad = grads * (z * horner(W_POLY, z))
-    return weight_grad.astype(jnp.bfloat16), jnp.sum(weight_grad * u)
+    soft = u - r * ((0.25 - z) * horner(F_POLY, z))
+    wave = z * horner(W_POLY, z)
+    return tuple(t.astype(jnp.bfloat16) for t in (scale * soft, wave, soft - u * wave))
+
+
+def quant_grads(wave, slope, grads):
+    weight_grad = grads * wave.astype(jnp.float32)
+    return weight_grad.astype(jnp.bfloat16), jnp.sum(grads * slope.astype(jnp.float32))
 
 
 def dot(a, b, dims=(((1,), (0,)), ((), ()))):
@@ -98,12 +98,14 @@
             distance *= 2
         return value
 
+    def columns_of(value, part):
+        if parts == 2:
+            return jnp.where(part == 0, value[:, :part_width], value[:, part_width:])
+        return lax.dynamic_slice_in_dim(value, part * part_width, part_width, axis=1)
+
     def spread(value):
-        pieces = []
-        for k in range(parts):
-            start = (part_id ^ k) * part_width
-            piece = lax.dynamic_slice_in_dim(value, start, part_width, axis=1)
-            pieces.append(swap(piece, k) if k else piece)
+        pieces = [columns_of(value, part_id ^ k) for k in range(parts)]
+        pieces = [swap(piece, k) if k else piece for k, piece in enumerate(pieces)]
         return jnp.concatenate(pieces, axis=0)
 
     def share(value):
@@ -136,33 +138,20 @@
                 columns.append(column)
         return jnp.concatenate(columns, axis=1)
 
-    def one_hots(routes):
+    def slot_hots(routes):
         near = jnp.bitwise_xor(routes, expert_id)
-        matches = (near[:, :, None] == jnp.arange(EXPERTS)).astype(jnp.float32)
-        both = matches.sum(1)
-        lower = (jnp.arange(tokens)[:, None] > jnp.arange(tokens)[None, :]).astype(jnp.float32)
-        earlier = dot(lower, both)
-        chosen, seen = [], earlier
+        matches = (near[:, :, None] == jnp.arange(EXPERTS)).astype(jnp.bfloat16)
+        place = jnp.arange(parts * tokens)
+        block = place // tokens
+        ahead = (place[:, None] > place[None, :]) & (block[:, None] == block[None, :])
+        earlier = dot(ahead.astype(jnp.bfloat16), matches.sum(1).astype(jnp.bfloat16))
+        first = jnp.bitwise_xor(block, part_id) * CAP
+        hots = []
         for j in range(routes.shape[1]):
-            m = matches[:, j]
-            slot = jnp.sum(m * seen, axis=1)
-            at_slot = (slot[:, None] == jnp.arange(CAP, dtype=jnp.float32)).astype(jnp.float32)
-            chosen.append(m[:, :, None] * at_slot[:, None, :])
-            seen = seen + m
-        return chosen
-
-    def group_hots(routes):
-        hots = []
-        for block in range(parts):
-            hots.append(one_hots(routes[block * tokens : (block + 1) * tokens]))
-        out = []
-        for j in range(routes.shape[1]):
-            rows = []
-            for block in range(parts):
-                here = (jnp.arange(parts) == (part_id ^ block)).astype(jnp.float32)
-                rows.append(hots[block][j][:, :, None, :] * here[None, None, :, None])
-            out.append(jnp.concatenate(rows, axis=0).reshape(parts * tokens, -1))
-        return out
+            slot = jnp.sum(matches[:, j].astype(jnp.float32) * earlier, axis=1).astype(jnp.int32)
+            row = near[:, j] * (parts * CAP) + first + slot
+            hots.append(row[:, None] == jnp.arange(EXPERTS * parts * CAP))
+        return hots
 
     def pack(hot, values):
         return dot(hot, values, FIRST)
@@ -180,45 +169,48 @@
         wide = x.astype(jnp.float32)
         return lax.rsqrt(jnp.mean(wide * wide, axis=-1, keepdims=True) + epsilon)
 
-    small = jnp.concatenate(
-        [
-            routes_b[0].astype(jnp.float32),
-            gates_b[0],
-            inv_rms(acts_b[0]),
-            routes_a[0].astype(jnp.float32),
-            gates_a[0],
-            inv_rms(acts_a[0]),
-        ],
-        axis=1,
-    )
-    small = share(small)
     top = routes_a.shape[2]
-    routes_gb, gates_gb, rms_b, routes_ga, gates_ga, rms_a = jnp.split(
-        small, [top, 2 * top, 2 * top + 1, 3 * top + 1, 4 * top + 1], axis=1
-    )
-    x_b, c_b, x_a = spread(acts_b[0]), spread(cot_b[0]), spread(acts_a[0])
-
-    hots_b = group_hots(routes_gb.astype(jnp.int32))
-    hot_b = sum(hots_b).astype(jnp.bfloat16)
-    gate_b = sum(jnp.sum(h * gates_gb[:, j : j + 1], axis=0) for j, h in enumerate(hots_b))
-    norm_b = (x_b.astype(jnp.float32) * rms_b).astype(jnp.bfloat16)
+    small = share(jnp.concatenate([routes_b[0].astype(jnp.float32), gates_b[0]], axis=1))
+    routes_gb, gates_gb = small[:, :top], small[:, top:]
+    own_rms_b = inv_rms(acts_b[0])
+    norm_b = spread((acts_b[0].astype(jnp.float32) * own_rms_b).astype(jnp.bfloat16))
+    c_b = spread(cot_b[0])
+
+    hots_b = slot_hots(routes_gb.astype(jnp.int32))
+    hot_b = sum(h.astype(jnp.bfloat16) for h in hots_b)
     send_u = pack(hot_b, norm_b).astype(jnp.bfloat16)
     rows_u = jnp.concatenate(exchange(split(send_u)), axis=0)
+    gate_b = sum(
+        jnp.sum(jnp.where(h, gates_gb[:, j : j + 1], 0.0), axis=0) for j, h in enumerate(hots_b)
+    )
     send_c = (pack(hot_b, after(c_b, send_u)) * gate_b[:, None]).astype(jnp.bfloat16)
-    rows_c = jnp.concatenate(exchange(split(send_c)), axis=0)
-
-    q_up = fake_quant(after(w_up, send_c), s_up, inv_up)
-    q_down = fake_quant(after(w_down, q_up), s_down, inv_down)
-    x_a = after(x_a, q_down)
-    hots_a = [h.astype(jnp.bfloat16) for h in group_hots(routes_ga.astype(jnp.int32))]
+    blocks_c = exchange(split(send_c))
+
+    later_b, later_a, routes_a, gates_a, own_rms_b = after(
+        (acts_b[0], acts_a[0], routes_a[0], gates_a[0], own_rms_b), send_c
+    )
+    small = jnp.concatenate(
+        [routes_a.astype(jnp.float32), gates_a, inv_rms(later_a), own_rms_b], axis=1
+    )
+    small = share(small)
+    x_a, x_b = spread(later_a), spread(later_b)
+    routes_ga, gates_ga, rms_a, rms_b = jnp.split(small, [top, 2 * top, 2 * top + 1], axis=1)
+
+    q_up, *slopes_up = fake_quant(after(w_up, send_c), s_up, inv_up)
+    q_down, *slopes_down = fake_quant(after(w_down, q_up), s_down, inv_down)
+    x_a = after(x_a, q_up)
+    hots_a = [h.astype(jnp.bfloat16) for h in slot_hots(routes_ga.astype(jnp.int32))]
     norm_a = (x_a.astype(jnp.float32) * rms_a).astype(jnp.bfloat16)
     send_a = pack(sum(hots_a), norm_a).astype(jnp.bfloat16)
     blocks_a = exchange(split(send_a))
 
-    q_up, q_down = lax.optimization_barrier((q_up, q_down, send_a))[:2]
+    q_up, q_down, slopes_up, slopes_down = lax.optimization_barrier(
+        (q_up, q_down, slopes_up, slopes_down, send_a)
+    )[:4]
 
     own_pre_b = dot(rows_u, q_up)
     pre_b = rounded(part_sum(own_pre_b))
+    rows_c = jnp.concatenate(after(blocks_c, pre_b), axis=0)
     own_grad = dot(rows_c, q_down, LAST)
     hidden_grad = rounded(part_sum(own_grad))
     sigma = jax.nn.sigmoid(pre_b)
@@ -227,16 +219,11 @@
     input_rows = dot(pre_grad, q_up, LAST).astype(jnp.bfloat16)
     back = jnp.concatenate(exchange(split(input_rows)), axis=0)
 
-    rows_u, rows_c, own_pre_b, own_grad = lax.optimization_barrier(
-        (rows_u, rows_c, own_pre_b, own_grad, input_rows)
-    )[:4]
-    dw_up, sum_up = quant_grads(w_up, inv_up, dot(rows_u, pre_grad, FIRST))
-    dw_down, sum_down = quant_grads(w_down, inv_down, dot(hidden_b, rows_c, FIRST))
-    quant_up = jnp.sum(pre_grad.astype(jnp.float32) * own_pre_b)
-    quant_down = jnp.sum(hidden_b.astype(jnp.float32) * own_grad)
+    rows_u, rows_c = lax.optimization_barrier((rows_u, rows_c, input_rows))[:2]
+    dw_up, sum_up = quant_grads(*slopes_up, dot(rows_u, pre_grad, FIRST))
+    dw_down, sum_down = quant_grads(*slopes_down, dot(hidden_b, rows_c, FIRST))
     root = math.sqrt(w_up.size * parts * qlimit)
-    ds_up = (quant_up * inv_up - sum_up) / root
-    ds_down = (quant_down * inv_down - sum_down) / root
+    ds_up, ds_down = sum_up / root, sum_down / root
     sums = jnp.stack([is_mine * ds_up, is_mine * ds_down])
     for c in range(peers.bit_length() - 1):
         sums = sums + swap(sums, 1 << c)
@@ -245,11 +232,13 @@
     own_pre_a = dot(rows_a, q_up)
     pre_a = rounded(part_sum(own_pre_a))
     hidden_a = (pre_a * jax.nn.sigmoid(pre_a)).astype(jnp.bfloat16)
-    pieces = CHUNKS
-    step = part_width // pieces
+    lanes = 128 if part_width % 128 == 0 and part_width >= 128 * CHUNKS else 1
+    units = part_width // lanes
+    edges = [lanes * (-(-units * c // CHUNKS)) for c in range(CHUNKS + 1)]
+    spans = list(zip(edges[:-1], edges[1:]))
     chunks = []
-    for c in range(pieces):
-        outputs = dot(hidden_a, q_down[:, c * step : (c + 1) * step]).astype(jnp.bfloat16)
+    for low, high in spans:
+        outputs = dot(hidden_a, q_down[:, low:high]).astype(jnp.bfloat16)
         chunks.append(exchange(split(outputs)))
 
     grad = dot(hot_b, back)
@@ -261,9 +250,9 @@
     next_cot = in_columns([pass_on(grad_in.astype(jnp.bfloat16), -1)])
 
     passed = []
-    for c in range(pieces):
+    for c, (low, high) in enumerate(spans):
         done_a = jnp.concatenate(chunks[c], axis=0)
-        mixed = x_a[:, c * step : (c + 1) * step].astype(jnp.float32)
+        mixed = x_a[:, low:high].astype(jnp.float32)
         for j, h in enumerate(hots_a):
             mixed = mixed + gates_ga[:, j : j + 1] * dot(h, done_a)
         passed.append(pass_on(mixed.astype(jnp.bfloat16), 1))

time: 322 us -> 352 us (1.093)
  the two profiles are of different devices: /device:TPU:0 before, /device:TPU:13 now
where the time goes in v1:
time: 352 us; the launch traced here: 345 us
  waiting for transfers between devices  147 us (42%)
  starting transfers between devices  81.6 us (23%)
  other arithmetic  52.9 us (15%)
  matrix products  50.6 us (14%)
  local copies, waits for them, and re-layouts  8.51 us (2%)
  between operations  4.46 us (1%)
    ppermute x34, waiting for transfers between devices, swap(): lax.ppermute(value, 'expert', [(i, i ^ distance) for i in range(peers)])  123 us
    ppermute x34, starting transfers between devices, swap(): lax.ppermute(value, 'expert', [(i, i ^ distance) for i in range(peers)])  53.7 us
    dot_general x21, matrix products, dot(): return lax.dot_general(a, b, dims, preferred_element_type=jnp.float32)  50.6 us
    convert_element_type x2, other arithmetic, fake_quant(): t.astype(jnp.bfloat16)  37.5 us
    ppermute x8, starting transfers between devices, pass_on(): pieces.append(lax.ppermute(block, ('pipe', 'expert'), pairs))  27.9 us
    ppermute x8, waiting for transfers between devices, pass_on(): pieces.append(lax.ppermute(block, ('pipe', 'expert'), pairs))  23.5 us
  transfers between devices with their start and end apart: 42, of which 24 were waited for; matrix products, arithmetic and copies ran while one was open for 27% of the time, Pallas kernels for 0%

profile of v1, /device:TPU:13, one launch (start us, length us, event | category | flops | bytes accessed | tf_op | source)
XLA Modules:
  0.0 345.1 jit_solution(2863283917051707869)
XLA Ops:
  14.6 18.4 %subtract_convert_fusion.1 = (bf16[3584,1024]{1,0:T(8,128)(2,1)}, bf16[3584,1024]{1,0:T(8,128)(2,1)}, bf16[3584,1024]{1,0:T(8,128)(2,1)S(1)}) fusion(bf16[3584,1024]{1,0:T(8,128)(2,1)S(1)} %bitcast.104, f32[]{:T(128)S(6)} %div.62, f32[]{:T(128)} %fusion.89), kind=kLoop, calls=%fused_computation.8 | loop fusion | flops 128450560 | bytes 29360136 | tf_op jit(solution)/shard_map/convert_element_type | solution.py:37
  36.6 19.0 %subtract_convert_fusion = (bf16[1024,3584]{1,0:T(8,128)(2,1)}, bf16[1024,3584]{1,0:T(8,128)(2,1)}, bf16[1024,3584]{1,0:T(8,128)(2,1)}) fusion(bf16[1024,3584]{1,0:T(8,128)(2,1)S(1)} %bitcast.107, f32[]{:T(128)S(6)} %div.64, f32[]{:T(128)} %fusion.90), kind=kLoop, calls=%fused_computation.6 | loop fusion | flops 128450560 | bytes 29360136 | tf_op jit(solution)/shard_map/convert_element_type | solution.py:37
  59.5 19.2 %collective-permute-done.9 = bf16[68,3584]{1,0:T(8,128)(2,1)S(1)} collective-permute-done((bf16[68,3584]{1,0:T(8,128)(2,1)S(1)}, bf16[68,3584]{1,0:T(8,128)(2,1)S(1)}, u32[]{:S(2)}, u32[]{:S(2)}) %collective-permute-start.9) | collective-permute-done | bytes 487456 | tf_op jit(solution)/shard_map/ppermute | solution.py:84
  88.8 18.6 %collective-permute-done.11 = bf16[68,3584]{1,0:T(8,128)(2,1)} collective-permute-done((bf16[68,3584]{1,0:T(8,128)(2,1)}, bf16[68,3584]{1,0:T(8,128)(2,1)}, u32[]{:S(2)}, u32[]{:S(2)}) %collective-permute-start.11) | collective-permute-done | bytes 487456 | tf_op jit(solution)/shard_map/ppermute | solution.py:84
  107.4 12.5 %collective-permute-done.12 = bf16[68,3584]{1,0:T(8,128)(2,1)} collective-permute-done((bf16[68,3584]{1,0:T(8,128)(2,1)}, bf16[68,3584]{1,0:T(8,128)(2,1)}, u32[]{:S(2)}, u32[]{:S(2)}) %collective-permute-start.12) | collective-permute-done | bytes 487456 | tf_op jit(solution)/shard_map/ppermute | solution.py:84
  119.9 12.2 %collective-permute-done.13 = bf16[68,3584]{1,0:T(8,128)(2,1)} collective-permute-done((bf16[68,3584]{1,0:T(8,128)(2,1)}, bf16[68,3584]{1,0:T(8,128)(2,1)}, u32[]{:S(2)}, u32[]{:S(2)}) %collective-permute-start.13) | collective-permute-done | bytes 487456 | tf_op jit(solution)/shard_map/ppermute | solution.py:84
  133.9 6.0 %fusion.123 = f32[272,1024]{1,0:T(8,128)S(1)} fusion(bf16[272,3584]{1,0:T(8,128)(2,1)S(1)} %pad_maximum_fusion.1, bf16[1024,3584]{1,0:T(8,128)(2,1)} %get-tuple-element.44), kind=kOutput, calls=%fused_computation.238 | convolution fusion | flops 1996488704 | bytes 10403840 | tf_op jit(solution)/shard_map/dot_general | solution.py:46
  151.5 12.7 %multiply_reduce_fusion = (f32[]{:T(128)}, bf16[1024,3584]{1,0:T(8,128)(2,1)}) fusion(bf16[1024,3584]{1,0:T(8,128)(2,1)} %get-tuple-element.55, bf16[1024,3584]{1,0:T(8,128)(2,1)} %get-tuple-element.48, bf16[272,3584]{1,0:T(8,128)(2,1)} %copy-done.9, f32[272,1024]{1,0:T(8,128)S(1)} %add_reduce-precision_fusion), kind=kOutput, calls=%fused_computation.2 | convolution fusion | flops 2019901440 | bytes 25083908 | tf_op jit(solution)/shard_map/dot_general | solution.py:46
  169.0 10.6 %multiply_reduce_fusion.1 = (f32[]{:T(128)}, bf16[3584,1024]{1,0:T(8,128)(2,1)}) fusion(bf16[3584,1024]{1,0:T(8,128)(2,1)S(1)} %bitcast.113, bf16[3584,1024]{1,0:T(8,128)(2,1)S(1)} %bitcast.115, bf16[272,3584]{1,0:T(8,128)(2,1)} %copy-done.8, bf16[272,1024]{1,0:T(8,128)(2,1)} %copy-done.15), kind=kOutput, calls=%fused_computation.3 | convolution fusion | flops 2018508800 | bytes 24526852 | tf_op jit(solution)/shard_map/dot_general | solution.py:46
  180.9 10.0 %collective-permute-done.7 = bf16[68,3584]{1,0:T(8,128)(2,1)} collective-permute-done((bf16[68,3584]{1,0:T(8,128)(2,1)}, bf16[68,3584]{1,0:T(8,128)(2,1)}, u32[]{:S(2)}, u32[]{:S(2)}) %collective-permute-start.7) | collective-permute-done | bytes 487456 | tf_op jit(solution)/shard_map/ppermute | solution.py:84
  190.9 24.8 %collective-permute-start.39 = (f32[2,4]{1,0:T(2,128)S(1)}, f32[2,4]{1,0:T(2,128)S(1)}, u32[]{:S(2)}, u32[]{:S(2)}) collective-permute-start(f32[2,4]{1,0:T(2,128)S(1)} %pad_maximum_fusion.18), channel_id=1, source_target_pairs={{0,1},{1,0},{2,3},{3,2},{4,5},{5,4},{6,7},{7,6},{8,9},{9,8},{10,11... | collective-permute-start | bytes 104 | tf_op jit(solution)/shard_map/ppermute | solution.py:84
  215.8 7.3 %collective-permute-done.33 = bf16[68,3584]{1,0:T(8,128)(2,1)} collective-permute-done((bf16[68,3584]{1,0:T(8,128)(2,1)}, bf16[68,3584]{1,0:T(8,128)(2,1)}, u32[]{:S(2)}, u32[]{:S(2)}) %collective-permute-start.33) | collective-permute-done | bytes 487456 | tf_op jit(solution)/shard_map/ppermute | solution.py:84
  223.0 12.1 %collective-permute-done.34 = bf16[68,3584]{1,0:T(8,128)(2,1)} collective-permute-done((bf16[68,3584]{1,0:T(8,128)(2,1)}, bf16[68,3584]{1,0:T(8,128)(2,1)}, u32[]{:S(2)}, u32[]{:S(2)}) %collective-permute-start.34) | collective-permute-done | bytes 487456 | tf_op jit(solution)/shard_map/ppermute | solution.py:84
  239.2 5.7 %fusion.16 = f32[272,1024]{1,0:T(8,128)S(1)} fusion(bf16[3584,1024]{1,0:T(8,128)(2,1)} %copy-done.1, bf16[68,3584]{1,0:T(8,128)(2,1)} %collective-permute-done.7, bf16[68,3584]{1,0:T(8,128)(2,1)} %collective-permute-done.6, bf16[68,3584]{1,0:T(8,128)(2,1)} %collective-permute-done.5, bf16[68,3584]{1,0:T(8,128)(2,1)S(1)} %copy-done.16), kind=kOutput, calls=%fused_computation.55 | convolution fusion | flops 2004287488 | bytes 10403840 | tf_op jit(solution)/shard_map/dot_general | solution.py:46
  246.9 3.3 collective-permute-start.37
  261.7 9.5 %collective-permute-done.38 = bf16[64,3584]{1,0:T(8,128)(2,1)S(1)} collective-permute-done((bf16[64,3584]{1,0:T(8,128)(2,1)S(1)}, bf16[64,3584]{1,0:T(8,128)(2,1)S(1)}, u32[]{:S(2)}, u32[]{:S(2)}) %collective-permute-start.38) | collective-permute-done | bytes 458784 | tf_op jit(solution)/shard_map/ppermute | solution.py:128
  281.7 3.3 collective-permute-done.28
  285.1 7.3 %collective-permute-done.29 = bf16[68,1152]{1,0:T(8,128)(2,1)S(1)} collective-permute-done((bf16[68,1152]{1,0:T(8,128)(2,1)S(1)}, bf16[68,1152]{1,0:T(8,128)(2,1)S(1)}, u32[]{:S(2)}, u32[]{:S(2)}) %collective-permute-start.29) | collective-permute-done | bytes 156704 | tf_op jit(solution)/shard_map/ppermute | solution.py:84
  295.6 6.7 %collective-permute-done.23 = bf16[68,1152]{1,0:T(8,128)(2,1)S(1)} collective-permute-done((bf16[68,1152]{1,0:T(8,128)(2,1)S(1)}, bf16[68,1152]{1,0:T(8,128)(2,1)S(1)}, u32[]{:S(2)}, u32[]{:S(2)}) %collective-permute-start.23) | collective-permute-done | bytes 156704 | tf_op jit(solution)/shard_map/ppermute | solution.py:84
  302.3 11.6 %collective-permute-start.30 = (bf16[64,1152]{1,0:T(8,128)(2,1)S(1)}, bf16[64,1152]{1,0:T(8,128)(2,1)S(1)}, u32[]{:S(2)}, u32[]{:S(2)}) collective-permute-start(bf16[64,1152]{1,0:T(8,128)(2,1)S(1)} %get-tuple-element.113), channel_id=1, source_target_pairs={{0,9},{1,8},{2,11},{3,10},{4,13},{5,12},{6,15},{7,14},{8,17},{9,16... | collective-permute-start | bytes 442376 | tf_op jit(solution)/shard_map/ppermute | solution.py:128
  317.5 4.8 %collective-permute-done.19 = bf16[68,1280]{1,0:T(8,128)(2,1)S(1)} collective-permute-done((bf16[68,1280]{1,0:T(8,128)(2,1)S(1)}, bf16[68,1280]{1,0:T(8,128)(2,1)S(1)}, u32[]{:S(2)}, u32[]{:S(2)}) %collective-permute-start.19) | collective-permute-done | bytes 174112 | tf_op jit(solution)/shard_map/ppermute | solution.py:84
  329.9 3.9 %collective-permute-done.20 = bf16[64,1280]{1,0:T(8,128)(2,1)S(1)} collective-permute-done((bf16[64,1280]{1,0:T(8,128)(2,1)S(1)}, bf16[64,1280]{1,0:T(8,128)(2,1)S(1)}, u32[]{:S(2)}, u32[]{:S(2)}) %collective-permute-start.20) | collective-permute-done | bytes 163872 | tf_op jit(solution)/shard_map/ppermute | solution.py:128
  337.4 3.1 collective-permute-done.25
  340.5 3.2 collective-permute-done.26
  (227 shorter events, 94.7 us)
Async XLA Ops:
  14.1 41.6 %collective-permute-start.4 = (f32[64,6]{0,1:T(8,128)S(1)}, f32[64,6]{0,1:T(8,128)S(1)}, u32[]{:S(2)}, u32[]{:S(2)}) collective-permute-start(f32[64,6]{0,1:T(8,128)S(1)} %pad_maximum_fusion.14), channel_id=1, source_target_pairs={{0,1},{1,0},{2,3},{3,2},{4,5},{5,4},{6,7},{7,6},{8,9},{9,8},{10,11... | collective-permute-start | bytes 4616 | tf_op jit(solution)/shard_map/ppermute | solution.py:84
  14.2 41.9 %collective-permute-start.3 = (bf16[64,3584]{1,0:T(8,128)(2,1)S(1)}, bf16[64,3584]{1,0:T(8,128)(2,1)S(1)}, u32[]{:S(2)}, u32[]{:S(2)}) collective-permute-start(bf16[64,3584]{1,0:T(8,128)(2,1)S(1)} %get-tuple-element.93), channel_id=1, source_target_pairs={{0,1},{1,0},{2,3},{3,2},{4,5},{5,4},{6,7},{7,6},{8,9},{9,8},{10,11... | collective-permute-start | bytes 1376264 | tf_op jit(solution)/shard_map/ppermute | solution.py:84
  33.1 24.7 %collective-permute-start.10 = (bf16[68,3584]{1,0:T(8,128)(2,1)S(1)}, bf16[68,3584]{1,0:T(8,128)(2,1)S(1)}, u32[]{:S(2)}, u32[]{:S(2)}) collective-permute-start(bf16[68,3584]{1,0:T(8,128)(2,1)S(1)} %get-tuple-element.79), channel_id=1, source_target_pairs={{0,6},{1,7},{2,4},{3,5},{4,2},{5,3},{6,0},{7,1},{8,14},{9,15},{10,... | collective-permute-start | bytes 1462280 | tf_op jit(solution)/shard_map/ppermute | solution.py:84
  34.4 25.1 %collective-permute-start.8 = (bf16[68,3584]{1,0:T(8,128)(2,1)S(1)}, bf16[68,3584]{1,0:T(8,128)(2,1)S(1)}, u32[]{:S(2)}, u32[]{:S(2)}) collective-permute-start(bf16[68,3584]{1,0:T(8,128)(2,1)S(1)} %get-tuple-element.81), channel_id=1, source_target_pairs={{0,2},{1,3},{2,0},{3,1},{4,6},{5,7},{6,4},{7,5},{8,10},{9,11},{10,... | collective-permute-start | bytes 1462280 | tf_op jit(solution)/shard_map/ppermute | solution.py:84
  36.6 42.1 %collective-permute-start.9 = (bf16[68,3584]{1,0:T(8,128)(2,1)S(1)}, bf16[68,3584]{1,0:T(8,128)(2,1)S(1)}, u32[]{:S(2)}, u32[]{:S(2)}) collective-permute-start(bf16[68,3584]{1,0:T(8,128)(2,1)S(1)} %get-tuple-element.80), channel_id=1, source_target_pairs={{0,4},{1,5},{2,6},{3,7},{4,0},{5,1},{6,2},{7,3},{8,12},{9,13},{10,... | collective-permute-start | bytes 1462280 | tf_op jit(solution)/shard_map/ppermute | solution.py:84
  83.5 23.9 %collective-permute-start.11 = (bf16[68,3584]{1,0:T(8,128)(2,1)}, bf16[68,3584]{1,0:T(8,128)(2,1)}, u32[]{:S(2)}, u32[]{:S(2)}) collective-permute-start(bf16[68,3584]{1,0:T(8,128)(2,1)} %get-tuple-element.76), channel_id=1, source_target_pairs={{0,2},{1,3},{2,0},{3,1},{4,6},{5,7},{6,4},{7,5},{8,10},{9,11},{10,... | collective-permute-start | bytes 1462280 | tf_op jit(solution)/shard_map/ppermute | solution.py:84
  85.6 34.3 %collective-permute-start.12 = (bf16[68,3584]{1,0:T(8,128)(2,1)}, bf16[68,3584]{1,0:T(8,128)(2,1)}, u32[]{:S(2)}, u32[]{:S(2)}) collective-permute-start(bf16[68,3584]{1,0:T(8,128)(2,1)} %get-tuple-element.75), channel_id=1, source_target_pairs={{0,4},{1,5},{2,6},{3,7},{4,0},{5,1},{6,2},{7,3},{8,12},{9,13},{10,... | collective-permute-start | bytes 1462280 | tf_op jit(solution)/shard_map/ppermute | solution.py:84
  86.6 45.5 %collective-permute-start.13 = (bf16[68,3584]{1,0:T(8,128)(2,1)}, bf16[68,3584]{1,0:T(8,128)(2,1)}, u32[]{:S(2)}, u32[]{:S(2)}) collective-permute-start(bf16[68,3584]{1,0:T(8,128)(2,1)} %get-tuple-element.74), channel_id=1, source_target_pairs={{0,6},{1,7},{2,4},{3,5},{4,2},{5,3},{6,0},{7,1},{8,14},{9,15},{10,... | collective-permute-start | bytes 1462280 | tf_op jit(solution)/shard_map/ppermute | solution.py:84
  142.1 73.7 %collective-permute-start.35 = (bf16[64,3584]{1,0:T(8,128)(2,1)}, bf16[64,3584]{1,0:T(8,128)(2,1)}, u32[]{:S(2)}, u32[]{:S(2)}) collective-permute-start(bf16[64,3584]{1,0:T(8,128)(2,1)} %get-tuple-element.91), channel_id=1, source_target_pairs={{0,1},{1,0},{2,3},{3,2},{4,5},{5,4},{6,7},{7,6},{8,9},{9,8},{10,11... | collective-permute-start | bytes 1376264 | tf_op jit(solution)/shard_map/ppermute | solution.py:84
  143.5 21.6 %collective-permute-start.5 = (bf16[68,3584]{1,0:T(8,128)(2,1)}, bf16[68,3584]{1,0:T(8,128)(2,1)}, u32[]{:S(2)}, u32[]{:S(2)}) collective-permute-start(bf16[68,3584]{1,0:T(8,128)(2,1)} %get-tuple-element.84), channel_id=1, source_target_pairs={{0,2},{1,3},{2,0},{3,1},{4,6},{5,7},{6,4},{7,5},{8,10},{9,11},{10,... | collective-permute-start | bytes 1462280 | tf_op jit(solution)/shard_map/ppermute | solution.py:84
  143.5 25.1 %collective-permute-start.6 = (bf16[68,3584]{1,0:T(8,128)(2,1)}, bf16[68,3584]{1,0:T(8,128)(2,1)}, u32[]{:S(2)}, u32[]{:S(2)}) collective-permute-start(bf16[68,3584]{1,0:T(8,128)(2,1)} %get-tuple-element.83), channel_id=1, source_target_pairs={{0,4},{1,5},{2,6},{3,7},{4,0},{5,1},{6,2},{7,3},{8,12},{9,13},{10,... | collective-permute-start | bytes 1462280 | tf_op jit(solution)/shard_map/ppermute | solution.py:84
  145.9 45.0 %collective-permute-start.7 = (bf16[68,3584]{1,0:T(8,128)(2,1)}, bf16[68,3584]{1,0:T(8,128)(2,1)}, u32[]{:S(2)}, u32[]{:S(2)}) collective-permute-start(bf16[68,3584]{1,0:T(8,128)(2,1)} %get-tuple-element.82), channel_id=1, source_target_pairs={{0,6},{1,7},{2,4},{3,5},{4,2},{5,3},{6,0},{7,1},{8,14},{9,15},{10,... | collective-permute-start | bytes 1462280 | tf_op jit(solution)/shard_map/ppermute | solution.py:84
  150.5 65.3 %collective-permute-start.32 = (bf16[68,3584]{1,0:T(8,128)(2,1)}, bf16[68,3584]{1,0:T(8,128)(2,1)}, u32[]{:S(2)}, u32[]{:S(2)}) collective-permute-start(bf16[68,3584]{1,0:T(8,128)(2,1)} %get-tuple-element.73), channel_id=1, source_target_pairs={{0,2},{1,3},{2,0},{3,1},{4,6},{5,7},{6,4},{7,5},{8,10},{9,11},{10,... | collective-permute-start | bytes 1462280 | tf_op jit(solution)/shard_map/ppermute | solution.py:84
  165.1 57.9 %collective-permute-start.33 = (bf16[68,3584]{1,0:T(8,128)(2,1)}, bf16[68,3584]{1,0:T(8,128)(2,1)}, u32[]{:S(2)}, u32[]{:S(2)}) collective-permute-start(bf16[68,3584]{1,0:T(8,128)(2,1)} %get-tuple-element.72), channel_id=1, source_target_pairs={{0,4},{1,5},{2,6},{3,7},{4,0},{5,1},{6,2},{7,3},{8,12},{9,13},{10,... | collective-permute-start | bytes 1462280 | tf_op jit(solution)/shard_map/ppermute | solution.py:84
  168.7 66.4 %collective-permute-start.34 = (bf16[68,3584]{1,0:T(8,128)(2,1)}, bf16[68,3584]{1,0:T(8,128)(2,1)}, u32[]{:S(2)}, u32[]{:S(2)}) collective-permute-start(bf16[68,3584]{1,0:T(8,128)(2,1)} %get-tuple-element.71), channel_id=1, source_target_pairs={{0,6},{1,7},{2,4},{3,5},{4,2},{5,3},{6,0},{7,1},{8,14},{9,15},{10,... | collective-permute-start | bytes 1462280 | tf_op jit(solution)/shard_map/ppermute | solution.py:84
  190.9 61.8 %collective-permute-start.39 = (f32[2,4]{1,0:T(2,128)S(1)}, f32[2,4]{1,0:T(2,128)S(1)}, u32[]{:S(2)}, u32[]{:S(2)}) collective-permute-start(f32[2,4]{1,0:T(2,128)S(1)} %pad_maximum_fusion.18), channel_id=1, source_target_pairs={{0,1},{1,0},{2,3},{3,2},{4,5},{5,4},{6,7},{7,6},{8,9},{9,8},{10,11... | collective-permute-start | bytes 104 | tf_op jit(solution)/shard_map/ppermute | solution.py:84
  245.0 27.2 %collective-permute-start.16 = (f32[272,1024]{1,0:T(8,128)S(1)}, f32[272,1024]{1,0:T(8,128)S(1)}, u32[]{:S(2)}, u32[]{:S(2)}) collective-permute-start(f32[272,1024]{1,0:T(8,128)S(1)} %fusion.16), channel_id=1, source_target_pairs={{0,1},{1,0},{2,3},{3,2},{4,5},{5,4},{6,7},{7,6},{8,9},{9,8},{10,11... | collective-permute-start | bytes 3342344 | tf_op jit(solution)/shard_map/ppermute | solution.py:84
  279.3 23.1 %collective-permute-start.23 = (bf16[68,1152]{1,0:T(8,128)(2,1)S(1)}, bf16[68,1152]{1,0:T(8,128)(2,1)S(1)}, u32[]{:S(2)}, u32[]{:S(2)}) collective-permute-start(bf16[68,1152]{1,0:T(8,128)(2,1)S(1)} %get-tuple-element.108), channel_id=1, source_target_pairs={{0,4},{1,5},{2,6},{3,7},{4,0},{5,1},{6,2},{7,3},{8,12},{9,13},{10,... | collective-permute-start | bytes 470024 | tf_op jit(solution)/shard_map/ppermute | solution.py:84
  280.8 33.6 %collective-permute-start.24 = (bf16[68,1152]{1,0:T(8,128)(2,1)S(1)}, bf16[68,1152]{1,0:T(8,128)(2,1)S(1)}, u32[]{:S(2)}, u32[]{:S(2)}) collective-permute-start(bf16[68,1152]{1,0:T(8,128)(2,1)S(1)} %get-tuple-element.107), channel_id=1, source_target_pairs={{0,6},{1,7},{2,4},{3,5},{4,2},{5,3},{6,0},{7,1},{8,14},{9,15},{10,... | collective-permute-start | bytes 470024 | tf_op jit(solution)/shard_map/ppermute | solution.py:84
  285.0 32.1 %collective-permute-start.17 = (bf16[68,1280]{1,0:T(8,128)(2,1)S(1)}, bf16[68,1280]{1,0:T(8,128)(2,1)S(1)}, u32[]{:S(2)}, u32[]{:S(2)}) collective-permute-start(bf16[68,1280]{1,0:T(8,128)(2,1)S(1)} %get-tuple-element.101), channel_id=1, source_target_pairs={{0,2},{1,3},{2,0},{3,1},{4,6},{5,7},{6,4},{7,5},{8,10},{9,11},{10,... | collective-permute-start | bytes 522248 | tf_op jit(solution)/shard_map/ppermute | solution.py:84
  292.3 25.2 %collective-permute-start.18 = (bf16[68,1280]{1,0:T(8,128)(2,1)S(1)}, bf16[68,1280]{1,0:T(8,128)(2,1)S(1)}, u32[]{:S(2)}, u32[]{:S(2)}) collective-permute-start(bf16[68,1280]{1,0:T(8,128)(2,1)S(1)} %get-tuple-element.100), channel_id=1, source_target_pairs={{0,4},{1,5},{2,6},{3,7},{4,0},{5,1},{6,2},{7,3},{8,12},{9,13},{10,... | collective-permute-start | bytes 522248 | tf_op jit(solution)/shard_map/ppermute | solution.py:84
  293.2 29.1 %collective-permute-start.19 = (bf16[68,1280]{1,0:T(8,128)(2,1)S(1)}, bf16[68,1280]{1,0:T(8,128)(2,1)S(1)}, u32[]{:S(2)}, u32[]{:S(2)}) collective-permute-start(bf16[68,1280]{1,0:T(8,128)(2,1)S(1)} %get-tuple-element.99), channel_id=1, source_target_pairs={{0,6},{1,7},{2,4},{3,5},{4,2},{5,3},{6,0},{7,1},{8,14},{9,15},{10,... | collective-permute-start | bytes 522248 | tf_op jit(solution)/shard_map/ppermute | solution.py:84
  302.3 41.3 %collective-permute-start.30 = (bf16[64,1152]{1,0:T(8,128)(2,1)S(1)}, bf16[64,1152]{1,0:T(8,128)(2,1)S(1)}, u32[]{:S(2)}, u32[]{:S(2)}) collective-permute-start(bf16[64,1152]{1,0:T(8,128)(2,1)S(1)} %get-tuple-element.113), channel_id=1, source_target_pairs={{0,9},{1,8},{2,11},{3,10},{4,13},{5,12},{6,15},{7,14},{8,17},{9,16... | collective-permute-start | bytes 442376 | tf_op jit(solution)/shard_map/ppermute | solution.py:128
  314.4 29.3 %collective-permute-start.31 = (bf16[64,1152]{1,0:T(8,128)(2,1)S(1)}, bf16[64,1152]{1,0:T(8,128)(2,1)S(1)}, u32[]{:S(2)}, u32[]{:S(2)}) collective-permute-start(bf16[64,1152]{1,0:T(8,128)(2,1)S(1)} %get-tuple-element.112), channel_id=1, source_target_pairs={{0,8},{1,9},{2,10},{3,11},{4,12},{5,13},{6,14},{7,15},{8,16},{9,17... | collective-permute-start | bytes 442376 | tf_op jit(solution)/shard_map/ppermute | solution.py:128
  (54 other events, 700.9 us)

commit v2 on v1

--- a/solution.py
+++ b/solution.py
@@ -217,7 +217,8 @@
     hidden_b = (pre_b * sigma).astype(jnp.bfloat16)
     pre_grad = (hidden_grad * sigma * (1.0 + pre_b * (1.0 - sigma))).astype(jnp.bfloat16)
     input_rows = dot(pre_grad, q_up, LAST).astype(jnp.bfloat16)
-    back = jnp.concatenate(exchange(split(input_rows)), axis=0)
+    blocks_back = exchange(split(input_rows))
+    back = jnp.concatenate(blocks_back, axis=0)
 
     rows_u, rows_c = lax.optimization_barrier((rows_u, rows_c, input_rows))[:2]
     dw_up, sum_up = quant_grads(*slopes_up, dot(rows_u, pre_grad, FIRST))
@@ -237,8 +238,10 @@
     edges = [lanes * (-(-units * c // CHUNKS)) for c in range(CHUNKS + 1)]
     spans = list(zip(edges[:-1], edges[1:]))
     chunks = []
-    for low, high in spans:
+    for c, (low, high) in enumerate(spans):
         outputs = dot(hidden_a, q_down[:, low:high]).astype(jnp.bfloat16)
+        if c == 0:
+            outputs = after(outputs, blocks_back[3])
         chunks.append(exchange(split(outputs)))
 
     grad = dot(hot_b, back)

time: 352 us -> 351 us (level)
  transfers between devices with their start and end apart: 42 -> 42, of which waited for: 24 -> 25; matrix products, arithmetic and copies ran while one was open for 27% -> 27% of each run, Pallas kernels for 0% -> 0%
where the time goes in v2:
time: 351 us; the launch traced here: 345 us
  waiting for transfers between devices  147 us (42%)
  starting transfers between devices  81.1 us (23%)
  other arithmetic  52.9 us (15%)
  matrix products  50.8 us (14%)
  local copies, waits for them, and re-layouts  8.47 us (2%)
  between operations  4.47 us (1%)
    ppermute x34, waiting for transfers between devices, swap(): lax.ppermute(value, 'expert', [(i, i ^ distance) for i in range(peers)])  124 us
    ppermute x34, starting transfers between devices, swap(): lax.ppermute(value, 'expert', [(i, i ^ distance) for i in range(peers)])  53.7 us
    dot_general x21, matrix products, dot(): return lax.dot_general(a, b, dims, preferred_element_type=jnp.float32)  50.8 us
    convert_element_type x2, other arithmetic, fake_quant(): t.astype(jnp.bfloat16)  37.5 us
    ppermute x8, starting transfers between devices, pass_on(): pieces.append(lax.ppermute(block, ('pipe', 'expert'), pairs))  27.4 us
    ppermute x8, waiting for transfers between devices, pass_on(): pieces.append(lax.ppermute(block, ('pipe', 'expert'), pairs))  22.8 us
  transfers between devices with their start and end apart: 42, of which 25 were waited for; matrix products, arithmetic and copies ran while one was open for 27% of the time, Pallas kernels for 0%

profile of v2, /device:TPU:13, one launch (start us, length us, event | category | flops | bytes accessed | tf_op | source)
XLA Modules:
  0.0 344.8 jit_solution(8500902134985321662)
XLA Ops:
  14.6 18.4 %subtract_convert_fusion.1 = (bf16[3584,1024]{1,0:T(8,128)(2,1)}, bf16[3584,1024]{1,0:T(8,128)(2,1)}, bf16[3584,1024]{1,0:T(8,128)(2,1)S(1)}) fusion(bf16[3584,1024]{1,0:T(8,128)(2,1)S(1)} %bitcast.104, f32[]{:T(128)S(6)} %div.62, f32[]{:T(128)} %fusion.89), kind=kLoop, calls=%fused_computation.8 | loop fusion | flops 128450560 | bytes 29360136 | tf_op jit(solution)/shard_map/convert_element_type | solution.py:37
  36.6 19.0 %subtract_convert_fusion = (bf16[1024,3584]{1,0:T(8,128)(2,1)}, bf16[1024,3584]{1,0:T(8,128)(2,1)}, bf16[1024,3584]{1,0:T(8,128)(2,1)}) fusion(bf16[1024,3584]{1,0:T(8,128)(2,1)S(1)} %bitcast.107, f32[]{:T(128)S(6)} %div.64, f32[]{:T(128)} %fusion.90), kind=kLoop, calls=%fused_computation.6 | loop fusion | flops 128450560 | bytes 29360136 | tf_op jit(solution)/shard_map/convert_element_type | solution.py:37
  59.5 19.2 %collective-permute-done.9 = bf16[68,3584]{1,0:T(8,128)(2,1)S(1)} collective-permute-done((bf16[68,3584]{1,0:T(8,128)(2,1)S(1)}, bf16[68,3584]{1,0:T(8,128)(2,1)S(1)}, u32[]{:S(2)}, u32[]{:S(2)}) %collective-permute-start.9) | collective-permute-done | bytes 487456 | tf_op jit(solution)/shard_map/ppermute | solution.py:84
  88.8 18.6 %collective-permute-done.11 = bf16[68,3584]{1,0:T(8,128)(2,1)} collective-permute-done((bf16[68,3584]{1,0:T(8,128)(2,1)}, bf16[68,3584]{1,0:T(8,128)(2,1)}, u32[]{:S(2)}, u32[]{:S(2)}) %collective-permute-start.11) | collective-permute-done | bytes 487456 | tf_op jit(solution)/shard_map/ppermute | solution.py:84
  107.4 12.5 %collective-permute-done.12 = bf16[68,3584]{1,0:T(8,128)(2,1)} collective-permute-done((bf16[68,3584]{1,0:T(8,128)(2,1)}, bf16[68,3584]{1,0:T(8,128)(2,1)}, u32[]{:S(2)}, u32[]{:S(2)}) %collective-permute-start.12) | collective-permute-done | bytes 487456 | tf_op jit(solution)/shard_map/ppermute | solution.py:84
  119.9 12.2 %collective-permute-done.13 = bf16[68,3584]{1,0:T(8,128)(2,1)} collective-permute-done((bf16[68,3584]{1,0:T(8,128)(2,1)}, bf16[68,3584]{1,0:T(8,128)(2,1)}, u32[]{:S(2)}, u32[]{:S(2)}) %collective-permute-start.13) | collective-permute-done | bytes 487456 | tf_op jit(solution)/shard_map/ppermute | solution.py:84
  133.9 6.0 %fusion.123 = f32[272,1024]{1,0:T(8,128)S(1)} fusion(bf16[272,3584]{1,0:T(8,128)(2,1)S(1)} %pad_maximum_fusion.1, bf16[1024,3584]{1,0:T(8,128)(2,1)} %get-tuple-element.45), kind=kOutput, calls=%fused_computation.238 | convolution fusion | flops 1996488704 | bytes 10403840 | tf_op jit(solution)/shard_map/dot_general | solution.py:46
  151.7 12.8 %multiply_reduce_fusion = (f32[]{:T(128)}, bf16[1024,3584]{1,0:T(8,128)(2,1)}) fusion(bf16[1024,3584]{1,0:T(8,128)(2,1)} %get-tuple-element.57, bf16[1024,3584]{1,0:T(8,128)(2,1)} %get-tuple-element.49, bf16[272,3584]{1,0:T(8,128)(2,1)} %copy-done.9, f32[272,1024]{1,0:T(8,128)S(1)} %add_reduce-precision_fusion), kind=kOutput, calls=%fused_computation.2 | convolution fusion | flops 2019901440 | bytes 25083908 | tf_op jit(solution)/shard_map/dot_general | solution.py:46
  168.7 10.6 %multiply_reduce_fusion.1 = (f32[]{:T(128)}, bf16[3584,1024]{1,0:T(8,128)(2,1)}) fusion(bf16[3584,1024]{1,0:T(8,128)(2,1)S(1)} %bitcast.113, bf16[3584,1024]{1,0:T(8,128)(2,1)S(1)} %bitcast.115, bf16[272,3584]{1,0:T(8,128)(2,1)} %copy-done.8, bf16[272,1024]{1,0:T(8,128)(2,1)} %copy-done.15), kind=kOutput, calls=%fused_computation.3 | convolution fusion | flops 2018508800 | bytes 24526852 | tf_op jit(solution)/shard_map/dot_general | solution.py:46
  180.7 21.3 %collective-permute-done.7 = bf16[68,3584]{1,0:T(8,128)(2,1)} collective-permute-done((bf16[68,3584]{1,0:T(8,128)(2,1)}, bf16[68,3584]{1,0:T(8,128)(2,1)}, u32[]{:S(2)}, u32[]{:S(2)}) %collective-permute-start.7) | collective-permute-done | bytes 487456 | tf_op jit(solution)/shard_map/ppermute | solution.py:84
  202.0 13.8 %collective-permute-start.39 = (f32[2,4]{1,0:T(2,128)S(1)}, f32[2,4]{1,0:T(2,128)S(1)}, u32[]{:S(2)}, u32[]{:S(2)}) collective-permute-start(f32[2,4]{1,0:T(2,128)S(1)} %pad_maximum_fusion.18), channel_id=1, source_target_pairs={{0,1},{1,0},{2,3},{3,2},{4,5},{5,4},{6,7},{7,6},{8,9},{9,8},{10,11... | collective-permute-start | bytes 104 | tf_op jit(solution)/shard_map/ppermute | solution.py:84
  215.8 8.3 %collective-permute-done.17 = bf16[68,3584]{1,0:T(8,128)(2,1)} collective-permute-done((bf16[68,3584]{1,0:T(8,128)(2,1)}, bf16[68,3584]{1,0:T(8,128)(2,1)}, u32[]{:S(2)}, u32[]{:S(2)}) %collective-permute-start.17) | collective-permute-done | bytes 487456 | tf_op jit(solution)/shard_map/ppermute | solution.py:84
  224.1 10.1 %collective-permute-done.34 = bf16[68,3584]{1,0:T(8,128)(2,1)} collective-permute-done((bf16[68,3584]{1,0:T(8,128)(2,1)}, bf16[68,3584]{1,0:T(8,128)(2,1)}, u32[]{:S(2)}, u32[]{:S(2)}) %collective-permute-start.34) | collective-permute-done | bytes 487456 | tf_op jit(solution)/shard_map/ppermute | solution.py:84
  238.2 5.7 %fusion.16 = f32[272,1024]{1,0:T(8,128)S(1)} fusion(bf16[3584,1024]{1,0:T(8,128)(2,1)} %copy-done.1, bf16[68,3584]{1,0:T(8,128)(2,1)} %collective-permute-done.7, bf16[68,3584]{1,0:T(8,128)(2,1)} %collective-permute-done.6, bf16[68,3584]{1,0:T(8,128)(2,1)} %collective-permute-done.5, bf16[68,3584]{1,0:T(8,128)(2,1)S(1)} %copy-done.16), kind=kOutput, calls=%fused_computation.55 | convolution fusion | flops 2004287488 | bytes 10403840 | tf_op jit(solution)/shard_map/dot_general | solution.py:46
  245.9 3.3 collective-permute-start.37
  260.6 9.5 %collective-permute-done.38 = bf16[64,3584]{1,0:T(8,128)(2,1)S(1)} collective-permute-done((bf16[64,3584]{1,0:T(8,128)(2,1)S(1)}, bf16[64,3584]{1,0:T(8,128)(2,1)S(1)}, u32[]{:S(2)}, u32[]{:S(2)}) %collective-permute-start.38) | collective-permute-done | bytes 458784 | tf_op jit(solution)/shard_map/ppermute | solution.py:128
  286.3 6.2 %collective-permute-done.30 = bf16[68,1152]{1,0:T(8,128)(2,1)S(1)} collective-permute-done((bf16[68,1152]{1,0:T(8,128)(2,1)S(1)}, bf16[68,1152]{1,0:T(8,128)(2,1)S(1)}, u32[]{:S(2)}, u32[]{:S(2)}) %collective-permute-start.30) | collective-permute-done | bytes 156704 | tf_op jit(solution)/shard_map/ppermute | solution.py:84
  293.3 7.5 %collective-permute-start.20 = (bf16[68,1280]{1,0:T(8,128)(2,1)S(1)}, bf16[68,1280]{1,0:T(8,128)(2,1)S(1)}, u32[]{:S(2)}, u32[]{:S(2)}) collective-permute-start(bf16[68,1280]{1,0:T(8,128)(2,1)S(1)} %get-tuple-element.101), channel_id=1, source_target_pairs={{0,6},{1,7},{2,4},{3,5},{4,2},{5,3},{6,0},{7,1},{8,14},{9,15},{10,... | collective-permute-start | bytes 522248 | tf_op jit(solution)/shard_map/ppermute | solution.py:84
  302.2 11.4 %collective-permute-start.31 = (bf16[64,1152]{1,0:T(8,128)(2,1)S(1)}, bf16[64,1152]{1,0:T(8,128)(2,1)S(1)}, u32[]{:S(2)}, u32[]{:S(2)}) collective-permute-start(bf16[64,1152]{1,0:T(8,128)(2,1)S(1)} %get-tuple-element.115), channel_id=1, source_target_pairs={{0,9},{1,8},{2,11},{3,10},{4,13},{5,12},{6,15},{7,14},{8,17},{9,16... | collective-permute-start | bytes 442376 | tf_op jit(solution)/shard_map/ppermute | solution.py:128
  317.4 4.9 %collective-permute-done.20 = bf16[68,1280]{1,0:T(8,128)(2,1)S(1)} collective-permute-done((bf16[68,1280]{1,0:T(8,128)(2,1)S(1)}, bf16[68,1280]{1,0:T(8,128)(2,1)S(1)}, u32[]{:S(2)}, u32[]{:S(2)}) %collective-permute-start.20) | collective-permute-done | bytes 174112 | tf_op jit(solution)/shard_map/ppermute | solution.py:84
  323.2 2.6 collective-permute-start.21
  329.7 3.9 %collective-permute-done.21 = bf16[64,1280]{1,0:T(8,128)(2,1)S(1)} collective-permute-done((bf16[64,1280]{1,0:T(8,128)(2,1)S(1)}, bf16[64,1280]{1,0:T(8,128)(2,1)S(1)}, u32[]{:S(2)}, u32[]{:S(2)}) %collective-permute-start.21) | collective-permute-done | bytes 163872 | tf_op jit(solution)/shard_map/ppermute | solution.py:128
  337.1 3.1 collective-permute-done.26
  340.3 3.2 collective-permute-done.27
  (227 shorter events, 96.1 us)
Async XLA Ops:
  14.1 41.6 %collective-permute-start.4 = (f32[64,6]{0,1:T(8,128)S(1)}, f32[64,6]{0,1:T(8,128)S(1)}, u32[]{:S(2)}, u32[]{:S(2)}) collective-permute-start(f32[64,6]{0,1:T(8,128)S(1)} %pad_maximum_fusion.14), channel_id=1, source_target_pairs={{0,1},{1,0},{2,3},{3,2},{4,5},{5,4},{6,7},{7,6},{8,9},{9,8},{10,11... | collective-permute-start | bytes 4616 | tf_op jit(solution)/shard_map/ppermute | solution.py:84
  14.2 41.9 %collective-permute-start.3 = (bf16[64,3584]{1,0:T(8,128)(2,1)S(1)}, bf16[64,3584]{1,0:T(8,128)(2,1)S(1)}, u32[]{:S(2)}, u32[]{:S(2)}) collective-permute-start(bf16[64,3584]{1,0:T(8,128)(2,1)S(1)} %get-tuple-element.95), channel_id=1, source_target_pairs={{0,1},{1,0},{2,3},{3,2},{4,5},{5,4},{6,7},{7,6},{8,9},{9,8},{10,11... | collective-permute-start | bytes 1376264 | tf_op jit(solution)/shard_map/ppermute | solution.py:84
  33.1 24.7 %collective-permute-start.10 = (bf16[68,3584]{1,0:T(8,128)(2,1)S(1)}, bf16[68,3584]{1,0:T(8,128)(2,1)S(1)}, u32[]{:S(2)}, u32[]{:S(2)}) collective-permute-start(bf16[68,3584]{1,0:T(8,128)(2,1)S(1)} %get-tuple-element.81), channel_id=1, source_target_pairs={{0,6},{1,7},{2,4},{3,5},{4,2},{5,3},{6,0},{7,1},{8,14},{9,15},{10,... | collective-permute-start | bytes 1462280 | tf_op jit(solution)/shard_map/ppermute | solution.py:84
  34.4 25.1 %collective-permute-start.8 = (bf16[68,3584]{1,0:T(8,128)(2,1)S(1)}, bf16[68,3584]{1,0:T(8,128)(2,1)S(1)}, u32[]{:S(2)}, u32[]{:S(2)}) collective-permute-start(bf16[68,3584]{1,0:T(8,128)(2,1)S(1)} %get-tuple-element.83), channel_id=1, source_target_pairs={{0,2},{1,3},{2,0},{3,1},{4,6},{5,7},{6,4},{7,5},{8,10},{9,11},{10,... | collective-permute-start | bytes 1462280 | tf_op jit(solution)/shard_map/ppermute | solution.py:84
  36.6 42.1 %collective-permute-start.9 = (bf16[68,3584]{1,0:T(8,128)(2,1)S(1)}, bf16[68,3584]{1,0:T(8,128)(2,1)S(1)}, u32[]{:S(2)}, u32[]{:S(2)}) collective-permute-start(bf16[68,3584]{1,0:T(8,128)(2,1)S(1)} %get-tuple-element.82), channel_id=1, source_target_pairs={{0,4},{1,5},{2,6},{3,7},{4,0},{5,1},{6,2},{7,3},{8,12},{9,13},{10,... | collective-permute-start | bytes 1462280 | tf_op jit(solution)/shard_map/ppermute | solution.py:84
  83.5 23.9 %collective-permute-start.11 = (bf16[68,3584]{1,0:T(8,128)(2,1)}, bf16[68,3584]{1,0:T(8,128)(2,1)}, u32[]{:S(2)}, u32[]{:S(2)}) collective-permute-start(bf16[68,3584]{1,0:T(8,128)(2,1)} %get-tuple-element.78), channel_id=1, source_target_pairs={{0,2},{1,3},{2,0},{3,1},{4,6},{5,7},{6,4},{7,5},{8,10},{9,11},{10,... | collective-permute-start | bytes 1462280 | tf_op jit(solution)/shard_map/ppermute | solution.py:84
  85.6 34.3 %collective-permute-start.12 = (bf16[68,3584]{1,0:T(8,128)(2,1)}, bf16[68,3584]{1,0:T(8,128)(2,1)}, u32[]{:S(2)}, u32[]{:S(2)}) collective-permute-start(bf16[68,3584]{1,0:T(8,128)(2,1)} %get-tuple-element.77), channel_id=1, source_target_pairs={{0,4},{1,5},{2,6},{3,7},{4,0},{5,1},{6,2},{7,3},{8,12},{9,13},{10,... | collective-permute-start | bytes 1462280 | tf_op jit(solution)/shard_map/ppermute | solution.py:84
  86.6 45.5 %collective-permute-start.13 = (bf16[68,3584]{1,0:T(8,128)(2,1)}, bf16[68,3584]{1,0:T(8,128)(2,1)}, u32[]{:S(2)}, u32[]{:S(2)}) collective-permute-start(bf16[68,3584]{1,0:T(8,128)(2,1)} %get-tuple-element.76), channel_id=1, source_target_pairs={{0,6},{1,7},{2,4},{3,5},{4,2},{5,3},{6,0},{7,1},{8,14},{9,15},{10,... | collective-permute-start | bytes 1462280 | tf_op jit(solution)/shard_map/ppermute | solution.py:84
  142.1 73.7 %collective-permute-start.35 = (bf16[64,3584]{1,0:T(8,128)(2,1)}, bf16[64,3584]{1,0:T(8,128)(2,1)}, u32[]{:S(2)}, u32[]{:S(2)}) collective-permute-start(bf16[64,3584]{1,0:T(8,128)(2,1)} %get-tuple-element.93), channel_id=1, source_target_pairs={{0,1},{1,0},{2,3},{3,2},{4,5},{5,4},{6,7},{7,6},{8,9},{9,8},{10,11... | collective-permute-start | bytes 1376264 | tf_op jit(solution)/shard_map/ppermute | solution.py:84
  143.5 21.6 %collective-permute-start.5 = (bf16[68,3584]{1,0:T(8,128)(2,1)}, bf16[68,3584]{1,0:T(8,128)(2,1)}, u32[]{:S(2)}, u32[]{:S(2)}) collective-permute-start(bf16[68,3584]{1,0:T(8,128)(2,1)} %get-tuple-element.86), channel_id=1, source_target_pairs={{0,2},{1,3},{2,0},{3,1},{4,6},{5,7},{6,4},{7,5},{8,10},{9,11},{10,... | collective-permute-start | bytes 1462280 | tf_op jit(solution)/shard_map/ppermute | solution.py:84
  143.5 25.1 %collective-permute-start.6 = (bf16[68,3584]{1,0:T(8,128)(2,1)}, bf16[68,3584]{1,0:T(8,128)(2,1)}, u32[]{:S(2)}, u32[]{:S(2)}) collective-permute-start(bf16[68,3584]{1,0:T(8,128)(2,1)} %get-tuple-element.85), channel_id=1, source_target_pairs={{0,4},{1,5},{2,6},{3,7},{4,0},{5,1},{6,2},{7,3},{8,12},{9,13},{10,... | collective-permute-start | bytes 1462280 | tf_op jit(solution)/shard_map/ppermute | solution.py:84
  145.9 56.1 %collective-permute-start.7 = (bf16[68,3584]{1,0:T(8,128)(2,1)}, bf16[68,3584]{1,0:T(8,128)(2,1)}, u32[]{:S(2)}, u32[]{:S(2)}) collective-permute-start(bf16[68,3584]{1,0:T(8,128)(2,1)} %get-tuple-element.84), channel_id=1, source_target_pairs={{0,6},{1,7},{2,4},{3,5},{4,2},{5,3},{6,0},{7,1},{8,14},{9,15},{10,... | collective-permute-start | bytes 1462280 | tf_op jit(solution)/shard_map/ppermute | solution.py:84
  150.5 73.6 %collective-permute-start.17 = (bf16[68,3584]{1,0:T(8,128)(2,1)}, bf16[68,3584]{1,0:T(8,128)(2,1)}, u32[]{:S(2)}, u32[]{:S(2)}) collective-permute-start(bf16[68,3584]{1,0:T(8,128)(2,1)} %get-tuple-element.75), channel_id=1, source_target_pairs={{0,6},{1,7},{2,4},{3,5},{4,2},{5,3},{6,0},{7,1},{8,14},{9,15},{10,... | collective-permute-start | bytes 1462280 | tf_op jit(solution)/shard_map/ppermute | solution.py:84
  165.1 59.0 %collective-permute-start.33 = (bf16[68,3584]{1,0:T(8,128)(2,1)}, bf16[68,3584]{1,0:T(8,128)(2,1)}, u32[]{:S(2)}, u32[]{:S(2)}) collective-permute-start(bf16[68,3584]{1,0:T(8,128)(2,1)} %get-tuple-element.74), channel_id=1, source_target_pairs={{0,2},{1,3},{2,0},{3,1},{4,6},{5,7},{6,4},{7,5},{8,10},{9,11},{10,... | collective-permute-start | bytes 1462280 | tf_op jit(solution)/shard_map/ppermute | solution.py:84
  168.7 65.4 %collective-permute-start.34 = (bf16[68,3584]{1,0:T(8,128)(2,1)}, bf16[68,3584]{1,0:T(8,128)(2,1)}, u32[]{:S(2)}, u32[]{:S(2)}) collective-permute-start(bf16[68,3584]{1,0:T(8,128)(2,1)} %get-tuple-element.73), channel_id=1, source_target_pairs={{0,4},{1,5},{2,6},{3,7},{4,0},{5,1},{6,2},{7,3},{8,12},{9,13},{10,... | collective-permute-start | bytes 1462280 | tf_op jit(solution)/shard_map/ppermute | solution.py:84
  202.0 49.7 %collective-permute-start.39 = (f32[2,4]{1,0:T(2,128)S(1)}, f32[2,4]{1,0:T(2,128)S(1)}, u32[]{:S(2)}, u32[]{:S(2)}) collective-permute-start(f32[2,4]{1,0:T(2,128)S(1)} %pad_maximum_fusion.18), channel_id=1, source_target_pairs={{0,1},{1,0},{2,3},{3,2},{4,5},{5,4},{6,7},{7,6},{8,9},{9,8},{10,11... | collective-permute-start | bytes 104 | tf_op jit(solution)/shard_map/ppermute | solution.py:84
  244.0 27.2 %collective-permute-start.16 = (f32[272,1024]{1,0:T(8,128)S(1)}, f32[272,1024]{1,0:T(8,128)S(1)}, u32[]{:S(2)}, u32[]{:S(2)}) collective-permute-start(f32[272,1024]{1,0:T(8,128)S(1)} %fusion.16), channel_id=1, source_target_pairs={{0,1},{1,0},{2,3},{3,2},{4,5},{5,4},{6,7},{7,6},{8,9},{9,8},{10,11... | collective-permute-start | bytes 3342344 | tf_op jit(solution)/shard_map/ppermute | solution.py:84
  280.4 21.8 %collective-permute-start.24 = (bf16[68,1152]{1,0:T(8,128)(2,1)S(1)}, bf16[68,1152]{1,0:T(8,128)(2,1)S(1)}, u32[]{:S(2)}, u32[]{:S(2)}) collective-permute-start(bf16[68,1152]{1,0:T(8,128)(2,1)S(1)} %get-tuple-element.110), channel_id=1, source_target_pairs={{0,4},{1,5},{2,6},{3,7},{4,0},{5,1},{6,2},{7,3},{8,12},{9,13},{10,... | collective-permute-start | bytes 470024 | tf_op jit(solution)/shard_map/ppermute | solution.py:84
  282.2 32.2 %collective-permute-start.25 = (bf16[68,1152]{1,0:T(8,128)(2,1)S(1)}, bf16[68,1152]{1,0:T(8,128)(2,1)S(1)}, u32[]{:S(2)}, u32[]{:S(2)}) collective-permute-start(bf16[68,1152]{1,0:T(8,128)(2,1)S(1)} %get-tuple-element.109), channel_id=1, source_target_pairs={{0,6},{1,7},{2,4},{3,5},{4,2},{5,3},{6,0},{7,1},{8,14},{9,15},{10,... | collective-permute-start | bytes 470024 | tf_op jit(solution)/shard_map/ppermute | solution.py:84
  285.1 32.1 %collective-permute-start.18 = (bf16[68,1280]{1,0:T(8,128)(2,1)S(1)}, bf16[68,1280]{1,0:T(8,128)(2,1)S(1)}, u32[]{:S(2)}, u32[]{:S(2)}) collective-permute-start(bf16[68,1280]{1,0:T(8,128)(2,1)S(1)} %get-tuple-element.103), channel_id=1, source_target_pairs={{0,2},{1,3},{2,0},{3,1},{4,6},{5,7},{6,4},{7,5},{8,10},{9,11},{10,... | collective-permute-start | bytes 522248 | tf_op jit(solution)/shard_map/ppermute | solution.py:84
  292.4 25.0 %collective-permute-start.19 = (bf16[68,1280]{1,0:T(8,128)(2,1)S(1)}, bf16[68,1280]{1,0:T(8,128)(2,1)S(1)}, u32[]{:S(2)}, u32[]{:S(2)}) collective-permute-start(bf16[68,1280]{1,0:T(8,128)(2,1)S(1)} %get-tuple-element.102), channel_id=1, source_target_pairs={{0,4},{1,5},{2,6},{3,7},{4,0},{5,1},{6,2},{7,3},{8,12},{9,13},{10,... | collective-permute-start | bytes 522248 | tf_op jit(solution)/shard_map/ppermute | solution.py:84
  293.3 29.0 %collective-permute-start.20 = (bf16[68,1280]{1,0:T(8,128)(2,1)S(1)}, bf16[68,1280]{1,0:T(8,128)(2,1)S(1)}, u32[]{:S(2)}, u32[]{:S(2)}) collective-permute-start(bf16[68,1280]{1,0:T(8,128)(2,1)S(1)} %get-tuple-element.101), channel_id=1, source_target_pairs={{0,6},{1,7},{2,4},{3,5},{4,2},{5,3},{6,0},{7,1},{8,14},{9,15},{10,... | collective-permute-start | bytes 522248 | tf_op jit(solution)/shard_map/ppermute | solution.py:84
  302.2 41.3 %collective-permute-start.31 = (bf16[64,1152]{1,0:T(8,128)(2,1)S(1)}, bf16[64,1152]{1,0:T(8,128)(2,1)S(1)}, u32[]{:S(2)}, u32[]{:S(2)}) collective-permute-start(bf16[64,1152]{1,0:T(8,128)(2,1)S(1)} %get-tuple-element.115), channel_id=1, source_target_pairs={{0,9},{1,8},{2,11},{3,10},{4,13},{5,12},{6,15},{7,14},{8,17},{9,16... | collective-permute-start | bytes 442376 | tf_op jit(solution)/shard_map/ppermute | solution.py:128
  314.4 29.0 %collective-permute-start.32 = (bf16[64,1152]{1,0:T(8,128)(2,1)S(1)}, bf16[64,1152]{1,0:T(8,128)(2,1)S(1)}, u32[]{:S(2)}, u32[]{:S(2)}) collective-permute-start(bf16[64,1152]{1,0:T(8,128)(2,1)S(1)} %get-tuple-element.114), channel_id=1, source_target_pairs={{0,8},{1,9},{2,10},{3,11},{4,12},{5,13},{6,14},{7,15},{8,16},{9,17... | collective-permute-start | bytes 442376 | tf_op jit(solution)/shard_map/ppermute | solution.py:128
  (54 other events, 700.7 us)

commit v3 on v2

--- a/solution.py
+++ b/solution.py
@@ -115,6 +115,9 @@
     def exchange(blocks):
         return [swap(b, k * parts) if k else b for k, b in enumerate(blocks)]
 
+    def ahead(value):
+        return lax.ppermute(value, "pipe", [(s, s + 1) for s in range(stages - 1)])
+
     def pass_on(value, by):
         pieces = []
         for k in range(parts):
@@ -198,11 +201,21 @@
 
     q_up, *slopes_up = fake_quant(after(w_up, send_c), s_up, inv_up)
     q_down, *slopes_down = fake_quant(after(w_down, q_up), s_down, inv_down)
+    lanes = 128 if part_width % 128 == 0 and part_width >= 128 * CHUNKS else 1
+    units = part_width // lanes
+    edges = [lanes * (-(-units * c // CHUNKS)) for c in range(CHUNKS + 1)]
+    spans = list(zip(edges[:-1], edges[1:]))
     x_a = after(x_a, q_up)
     hots_a = [h.astype(jnp.bfloat16) for h in slot_hots(routes_ga.astype(jnp.int32))]
+    low, high = spans[-1]
+    next_x = ahead(x_a[:, low:high])
+    routing = ahead(jnp.concatenate([routes_ga, gates_ga], axis=1))
+    next_hots = slot_hots(routing[:, :top].astype(jnp.int32))
+    sources = [(x_a[:, low:high], gates_ga, hots_a) for low, high in spans[:-1]]
+    sources.append((next_x, routing[:, top:], [h.astype(jnp.bfloat16) for h in next_hots]))
     norm_a = (x_a.astype(jnp.float32) * rms_a).astype(jnp.bfloat16)
     send_a = pack(sum(hots_a), norm_a).astype(jnp.bfloat16)
-    blocks_a = exchange(split(send_a))
+    blocks_a = exchange(split(after(send_a, blocks_c[-1])))
 
     q_up, q_down, slopes_up, slopes_down = lax.optimization_barrier(
         (q_up, q_down, slopes_up, slopes_down, send_a)
@@ -233,16 +246,13 @@
     own_pre_a = dot(rows_a, q_up)
     pre_a = rounded(part_sum(own_pre_a))
     hidden_a = (pre_a * jax.nn.sigmoid(pre_a)).astype(jnp.bfloat16)
-    lanes = 128 if part_width % 128 == 0 and part_width >= 128 * CHUNKS else 1
-    units = part_width // lanes
-    edges = [lanes * (-(-units * c // CHUNKS)) for c in range(CHUNKS + 1)]
-    spans = list(zip(edges[:-1], edges[1:]))
-    chunks = []
-    for c, (low, high) in enumerate(spans):
-        outputs = dot(hidden_a, q_down[:, low:high]).astype(jnp.bfloat16)
-        if c == 0:
-            outputs = after(outputs, blocks_back[3])
-        chunks.append(exchange(split(outputs)))
+    ready = [None] * CHUNKS
+    for c in (CHUNKS - 1, *range(CHUNKS - 1)):
+        low, high = spans[c]
+        ready[c] = dot(hidden_a, q_down[:, low:high]).astype(jnp.bfloat16)
+    ready[-1] = ahead(ready[-1])
+    ready[0] = after(ready[0], blocks_back[-1])
+    chunks = [exchange(split(rows)) for rows in ready]
 
     grad = dot(hot_b, back)
     x_wide = x_b.astype(jnp.float32)
@@ -253,12 +263,17 @@
     next_cot = in_columns([pass_on(grad_in.astype(jnp.bfloat16), -1)])
 
     passed = []
-    for c, (low, high) in enumerate(spans):
+    for c, (x_c, gates_c, hots_c) in enumerate(sources):
         done_a = jnp.concatenate(chunks[c], axis=0)
-        mixed = x_a[:, low:high].astype(jnp.float32)
-        for j, h in enumerate(hots_a):
-            mixed = mixed + gates_ga[:, j : j + 1] * dot(h, done_a)
-        passed.append(pass_on(mixed.astype(jnp.bfloat16), 1))
+        mixed = x_c.astype(jnp.float32)
+        for j, h in enumerate(hots_c):
+            mixed = mixed + gates_c[:, j : j + 1] * dot(h, done_a)
+        mixed = mixed.astype(jnp.bfloat16)
+        if c < CHUNKS - 1:
+            passed.append(pass_on(mixed, 1))
+        else:
+            pieces = jnp.split(mixed, parts, axis=0)
+            passed.append([swap(piece, k) if k else piece for k, piece in enumerate(pieces)])
     next_a = in_columns(passed)
     return (
         next_a[None],

time: 351 us -> 327 us (0.932)
  the two profiles are of different devices: /device:TPU:13 before, /device:TPU:0 now
where the time goes in v3:
time: 327 us
  starting transfers between devices  113 us (35%)
  waiting for transfers between devices  104 us (32%)
  matrix products  48.5 us (15%)
  other arithmetic  48.2 us (15%)
  local copies, waits for them, and re-layouts  8.66 us (3%)
  between operations  4.12 us (1%)
    ppermute x35, starting transfers between devices, swap(): lax.ppermute(value, 'expert', [(i, i ^ distance) for i in range(peers)])  88.2 us
    ppermute x35, waiting for transfers between devices, swap(): lax.ppermute(value, 'expert', [(i, i ^ distance) for i in range(peers)])  86.8 us
    dot_general x22, matrix products, dot(): return lax.dot_general(a, b, dims, preferred_element_type=jnp.float32)  48.5 us
    convert_element_type x2, other arithmetic, fake_quant(): t.astype(jnp.bfloat16)  36.8 us
    ppermute x6, waiting for transfers between devices, pass_on(): pieces.append(lax.ppermute(block, ('pipe', 'expert'), pairs))  17.5 us
    ppermute x6, starting transfers between devices, pass_on(): pieces.append(lax.ppermute(block, ('pipe', 'expert'), pairs))  13.1 us
    ppermute x3, starting transfers between devices, ahead(): return lax.ppermute(value, 'pipe', [(s, s + 1) for s in range(stages - 1)])  11.4 us
  transfers between devices with their start and end apart: 44, of which 19 were waited for; matrix products, arithmetic and copies ran while one was open for 24% of the time, Pallas kernels for 0%

profile of v3, /device:TPU:0, one launch (start us, length us, event | category | flops | bytes accessed | tf_op | source)
XLA Modules:
  0.0 326.5 jit_solution(7249540288094090477)
XLA Ops:
  15.3 18.5 %subtract_convert_fusion.1 = (bf16[3584,1024]{1,0:T(8,128)(2,1)S(1)}, bf16[3584,1024]{1,0:T(8,128)(2,1)}, bf16[3584,1024]{1,0:T(8,128)(2,1)S(1)}) fusion(bf16[3584,1024]{1,0:T(8,128)(2,1)S(1)} %bitcast.131, f32[]{:T(128)S(6)} %div.66, f32[]{:T(128)} %fusion.94), kind=kLoop, calls=%fused_computation.8 | loop fusion | flops 128450560 | bytes 29360136 | tf_op jit(solution)/shard_map/convert_element_type | solution.py:37
  34.4 4.7 %collective-permute-start.5 = (bf16[68,3584]{1,0:T(8,128)(2,1)}, bf16[68,3584]{1,0:T(8,128)(2,1)S(1)}, u32[]{:S(2)}, u32[]{:S(2)}) collective-permute-start(bf16[68,3584]{1,0:T(8,128)(2,1)} %get-tuple-element.83), channel_id=1, source_target_pairs={{0,6},{1,7},{2,4},{3,5},{4,2},{5,3},{6,0},{7,1},{8,14},{9,15},{10,... | collective-permute-start | bytes 1462280 | tf_op jit(solution)/shard_map/ppermute | solution.py:84
  40.1 18.3 %subtract_convert_fusion = (bf16[1024,3584]{1,0:T(8,128)(2,1)}, bf16[1024,3584]{1,0:T(8,128)(2,1)}, bf16[1024,3584]{1,0:T(8,128)(2,1)S(1)}) fusion(bf16[1024,3584]{1,0:T(8,128)(2,1)S(1)} %bitcast.134, f32[]{:T(128)S(6)} %div.68, f32[]{:T(128)} %fusion.95), kind=kLoop, calls=%fused_computation.6 | loop fusion | flops 128450560 | bytes 29360136 | tf_op jit(solution)/shard_map/convert_element_type | solution.py:37
  58.4 3.4 %collective-permute-start.9 = (bf16[68,3584]{1,0:T(8,128)(2,1)S(1)}, bf16[68,3584]{1,0:T(8,128)(2,1)S(1)}, u32[]{:S(2)}, u32[]{:S(2)}) collective-permute-start(bf16[68,3584]{1,0:T(8,128)(2,1)S(1)} %get-tuple-element.87), channel_id=1, source_target_pairs={{0,2},{1,3},{2,0},{3,1},{4,6},{5,7},{6,4},{7,5},{8,10},{9,11},{10,... | collective-permute-start | bytes 1462280 | tf_op jit(solution)/shard_map/ppermute | solution.py:84
  63.2 34.0 %collective-permute-start.13 = (bf16[68,3584]{1,0:T(8,128)(2,1)}, bf16[68,3584]{1,0:T(8,128)(2,1)S(1)}, u32[]{:S(2)}, u32[]{:S(2)}) collective-permute-start(bf16[68,3584]{1,0:T(8,128)(2,1)} %get-tuple-element.80), channel_id=1, source_target_pairs={{0,4},{1,5},{2,6},{3,7},{4,0},{5,1},{6,2},{7,3},{8,12},{9,13},{10,... | collective-permute-start | bytes 1462280 | tf_op jit(solution)/shard_map/ppermute | solution.py:84
  97.1 20.5 %collective-permute-done.10 = bf16[68,3584]{1,0:T(8,128)(2,1)S(1)} collective-permute-done((bf16[68,3584]{1,0:T(8,128)(2,1)S(1)}, bf16[68,3584]{1,0:T(8,128)(2,1)S(1)}, u32[]{:S(2)}, u32[]{:S(2)}) %collective-permute-start.10) | collective-permute-done | bytes 487456 | tf_op jit(solution)/shard_map/ppermute | solution.py:84
  117.7 3.6 %collective-permute-start.29 = (f32[128,4]{0,1:T(4,128)S(1)}, f32[128,4]{0,1:T(4,128)S(1)}, u32[]{:S(2)}, u32[]{:S(2)}) collective-permute-start(f32[128,4]{0,1:T(4,128)S(1)} %concatenate.77), channel_id=1, source_target_pairs={{0,8},{8,16},{16,24},{1,9},{9,17},{17,25},{2,10},{10,18},{18,26},{... | collective-permute-start | bytes 6152 | tf_op jit(solution)/shard_map/ppermute | solution.py:119
  128.5 3.2 fusion.130
  131.8 4.3 %collective-permute-start.28 = (bf16[128,1152]{1,0:T(8,128)(2,1)S(1)}, bf16[128,1152]{1,0:T(8,128)(2,1)}, u32[]{:S(2)}, u32[]{:S(2)}) collective-permute-start(bf16[128,1152]{1,0:T(8,128)(2,1)S(1)} %slice.172), channel_id=1, source_target_pairs={{0,8},{8,16},{16,24},{1,9},{9,17},{17,25},{2,10},{10,18},{18,26},{... | collective-permute-start | bytes 884744 | tf_op jit(solution)/shard_map/ppermute | solution.py:119
  137.4 3.0 collective-permute-start.7
  144.6 11.1 %multiply_reduce_fusion.1 = (f32[]{:T(128)}, bf16[3584,1024]{1,0:T(8,128)(2,1)}) fusion(bf16[3584,1024]{1,0:T(8,128)(2,1)S(1)} %get-tuple-element.58, bf16[3584,1024]{1,0:T(8,128)(2,1)} %get-tuple-element.49, bf16[272,3584]{1,0:T(8,128)(2,1)} %copy-done.4, bf16[272,1024]{1,0:T(8,128)(2,1)S(1)} %multiply_convert_fusion.7), kind=kOutput, calls=%fused_computation.3 | convolution fusion | flops 2018508800 | bytes 24526852 | tf_op jit(solution)/shard_map/dot_general | solution.py:46
  155.7 11.5 %multiply_reduce_fusion = (f32[]{:T(128)}, bf16[1024,3584]{1,0:T(8,128)(2,1)}) fusion(bf16[1024,3584]{1,0:T(8,128)(2,1)} %get-tuple-element.59, bf16[1024,3584]{1,0:T(8,128)(2,1)} %get-tuple-element.51, bf16[272,3584]{1,0:T(8,128)(2,1)S(1)} %copy-done.6, f32[272,1024]{1,0:T(8,128)S(1)} %add_reduce-precision_fusion), kind=kOutput, calls=%fused_computation.2 | convolution fusion | flops 2019901440 | bytes 25083908 | tf_op jit(solution)/shard_map/dot_general | solution.py:46
  168.7 6.9 %collective-permute-done.7 = bf16[68,3584]{1,0:T(8,128)(2,1)} collective-permute-done((bf16[68,3584]{1,0:T(8,128)(2,1)}, bf16[68,3584]{1,0:T(8,128)(2,1)}, u32[]{:S(2)}, u32[]{:S(2)}) %collective-permute-start.7) | collective-permute-done | bytes 487456 | tf_op jit(solution)/shard_map/ppermute | solution.py:84
  177.9 21.0 %collective-permute-start.36 = (bf16[68,3584]{1,0:T(8,128)(2,1)}, bf16[68,3584]{1,0:T(8,128)(2,1)}, u32[]{:S(2)}, u32[]{:S(2)}) collective-permute-start(bf16[68,3584]{1,0:T(8,128)(2,1)} %get-tuple-element.77), channel_id=1, source_target_pairs={{0,4},{1,5},{2,6},{3,7},{4,0},{5,1},{6,2},{7,3},{8,12},{9,13},{10,... | collective-permute-start | bytes 1462280 | tf_op jit(solution)/shard_map/ppermute | solution.py:84
  200.3 5.8 %fusion.10 = f32[272,1024]{1,0:T(8,128)S(1)} fusion(bf16[3584,1024]{1,0:T(8,128)(2,1)} %copy-done.2, bf16[68,3584]{1,0:T(8,128)(2,1)} %collective-permute-done.8, bf16[68,3584]{1,0:T(8,128)(2,1)} %collective-permute-done.7, bf16[68,3584]{1,0:T(8,128)(2,1)} %collective-permute-done.6, bf16[68,3584]{1,0:T(8,128)(2,1)S(1)} %copy-done.8), kind=kOutput, calls=%fused_computation.45 | convolution fusion | flops 2004287488 | bytes 10403840 | tf_op jit(solution)/shard_map/dot_general | solution.py:46
  206.2 26.1 %collective-permute-done.36 = bf16[68,3584]{1,0:T(8,128)(2,1)} collective-permute-done((bf16[68,3584]{1,0:T(8,128)(2,1)}, bf16[68,3584]{1,0:T(8,128)(2,1)}, u32[]{:S(2)}, u32[]{:S(2)}) %collective-permute-start.36) | collective-permute-done | bytes 487456 | tf_op jit(solution)/shard_map/ppermute | solution.py:84
  240.9 3.6 %collective-permute-done.42 = f32[2,4]{1,0:T(2,128)S(1)} collective-permute-done((f32[2,4]{1,0:T(2,128)S(1)}, f32[2,4]{1,0:T(2,128)S(1)}, u32[]{:S(2)}, u32[]{:S(2)}) %collective-permute-start.42) | collective-permute-done | bytes 64 | tf_op jit(solution)/shard_map/ppermute | solution.py:84
  245.5 3.6 %collective-permute-done.43 = f32[2,4]{1,0:T(2,128)S(1)} collective-permute-done((f32[2,4]{1,0:T(2,128)S(1)}, f32[2,4]{1,0:T(2,128)S(1)}, u32[]{:S(2)}, u32[]{:S(2)}) %collective-permute-start.43) | collective-permute-done | bytes 64 | tf_op jit(solution)/shard_map/ppermute | solution.py:84
  252.3 10.2 %collective-permute-done.40 = bf16[64,3584]{1,0:T(8,128)(2,1)S(1)} collective-permute-done((bf16[64,3584]{1,0:T(8,128)(2,1)S(1)}, bf16[64,3584]{1,0:T(8,128)(2,1)S(1)}, u32[]{:S(2)}, u32[]{:S(2)}) %collective-permute-start.40) | collective-permute-done | bytes 458784 | tf_op jit(solution)/shard_map/ppermute | solution.py:131
  277.9 12.3 %collective-permute-done.24 = bf16[68,1152]{1,0:T(8,128)(2,1)S(1)} collective-permute-done((bf16[68,1152]{1,0:T(8,128)(2,1)S(1)}, bf16[68,1152]{1,0:T(8,128)(2,1)S(1)}, u32[]{:S(2)}, u32[]{:S(2)}) %collective-permute-start.24) | collective-permute-done | bytes 156704 | tf_op jit(solution)/shard_map/ppermute | solution.py:84
  290.1 3.6 %collective-permute-start.30 = (bf16[272,1152]{1,0:T(8,128)(2,1)S(1)}, bf16[272,1152]{1,0:T(8,128)(2,1)S(1)}, u32[]{:S(2)}, u32[]{:S(2)}) collective-permute-start(bf16[272,1152]{1,0:T(8,128)(2,1)S(1)} %convolution_convert_fusion.4), channel_id=1, source_target_pairs={{0,8},{8,16},{16,24},{1,9},{9,17},{17,25},{2,10},{10,18},{18,26},{... | collective-permute-start | bytes 1880072 | tf_op jit(solution)/shard_map/ppermute | solution.py:119
  301.3 4.2 %collective-permute-start.22 = (bf16[64,1280]{1,0:T(8,128)(2,1)S(1)}, bf16[64,1280]{1,0:T(8,128)(2,1)S(1)}, u32[]{:S(2)}, u32[]{:S(2)}) collective-permute-start(bf16[64,1280]{1,0:T(8,128)(2,1)S(1)} %get-tuple-element.116), channel_id=1, source_target_pairs={{0,8},{1,9},{2,10},{3,11},{4,12},{5,13},{6,14},{7,15},{8,16},{9,17... | collective-permute-start | bytes 491528 | tf_op jit(solution)/shard_map/ppermute | solution.py:131
  314.7 3.4 %collective-permute-start.27 = (bf16[64,1152]{1,0:T(8,128)(2,1)S(1)}, bf16[64,1152]{1,0:T(8,128)(2,1)S(1)}, u32[]{:S(2)}, u32[]{:S(2)}) collective-permute-start(bf16[64,1152]{1,0:T(8,128)(2,1)S(1)} %get-tuple-element.118), channel_id=1, source_target_pairs={{0,8},{1,9},{2,10},{3,11},{4,12},{5,13},{6,14},{7,15},{8,16},{9,17... | collective-permute-start | bytes 442376 | tf_op jit(solution)/shard_map/ppermute | solution.py:131
  318.2 4.0 %collective-permute-done.32 = bf16[68,1152]{1,0:T(8,128)(2,1)S(1)} collective-permute-done((bf16[68,1152]{1,0:T(8,128)(2,1)S(1)}, bf16[68,1152]{1,0:T(8,128)(2,1)S(1)}, u32[]{:S(2)}, u32[]{:S(2)}) %collective-permute-start.32) | collective-permute-done | bytes 156704 | tf_op jit(solution)/shard_map/ppermute | solution.py:84
  (212 shorter events, 81.6 us)
Async XLA Ops:
  33.8 28.4 %collective-permute-start.3 = (bf16[64,3584]{1,0:T(8,128)(2,1)S(1)}, bf16[64,3584]{1,0:T(8,128)(2,1)S(1)}, u32[]{:S(2)}, u32[]{:S(2)}) collective-permute-start(bf16[64,3584]{1,0:T(8,128)(2,1)S(1)} %get-tuple-element.99), channel_id=1, source_target_pairs={{0,1},{1,0},{2,3},{3,2},{4,5},{5,4},{6,7},{7,6},{8,9},{9,8},{10,11... | collective-permute-start | bytes 1376264 | tf_op jit(solution)/shard_map/ppermute | solution.py:84
  33.9 24.5 %collective-permute-start.4 = (f32[64,6]{0,1:T(8,128)S(1)}, f32[64,6]{0,1:T(8,128)S(1)}, u32[]{:S(2)}, u32[]{:S(2)}) collective-permute-start(f32[64,6]{0,1:T(8,128)S(1)} %pad_maximum_fusion.14), channel_id=1, source_target_pairs={{0,1},{1,0},{2,3},{3,2},{4,5},{5,4},{6,7},{7,6},{8,9},{9,8},{10,11... | collective-permute-start | bytes 4616 | tf_op jit(solution)/shard_map/ppermute | solution.py:84
  34.4 92.5 %collective-permute-start.5 = (bf16[68,3584]{1,0:T(8,128)(2,1)}, bf16[68,3584]{1,0:T(8,128)(2,1)S(1)}, u32[]{:S(2)}, u32[]{:S(2)}) collective-permute-start(bf16[68,3584]{1,0:T(8,128)(2,1)} %get-tuple-element.83), channel_id=1, source_target_pairs={{0,6},{1,7},{2,4},{3,5},{4,2},{5,3},{6,0},{7,1},{8,14},{9,15},{10,... | collective-permute-start | bytes 1462280 | tf_op jit(solution)/shard_map/ppermute | solution.py:84
  39.1 24.1 %collective-permute-start.11 = (bf16[68,3584]{1,0:T(8,128)(2,1)}, bf16[68,3584]{1,0:T(8,128)(2,1)S(1)}, u32[]{:S(2)}, u32[]{:S(2)}) collective-permute-start(bf16[68,3584]{1,0:T(8,128)(2,1)} %get-tuple-element.85), channel_id=1, source_target_pairs={{0,6},{1,7},{2,4},{3,5},{4,2},{5,3},{6,0},{7,1},{8,14},{9,15},{10,... | collective-permute-start | bytes 1462280 | tf_op jit(solution)/shard_map/ppermute | solution.py:84
  39.2 78.5 %collective-permute-start.10 = (bf16[68,3584]{1,0:T(8,128)(2,1)S(1)}, bf16[68,3584]{1,0:T(8,128)(2,1)S(1)}, u32[]{:S(2)}, u32[]{:S(2)}) collective-permute-start(bf16[68,3584]{1,0:T(8,128)(2,1)S(1)} %get-tuple-element.86), channel_id=1, source_target_pairs={{0,4},{1,5},{2,6},{3,7},{4,0},{5,1},{6,2},{7,3},{8,12},{9,13},{10,... | collective-permute-start | bytes 1462280 | tf_op jit(solution)/shard_map/ppermute | solution.py:84
  58.4 62.8 %collective-permute-start.9 = (bf16[68,3584]{1,0:T(8,128)(2,1)S(1)}, bf16[68,3584]{1,0:T(8,128)(2,1)S(1)}, u32[]{:S(2)}, u32[]{:S(2)}) collective-permute-start(bf16[68,3584]{1,0:T(8,128)(2,1)S(1)} %get-tuple-element.87), channel_id=1, source_target_pairs={{0,2},{1,3},{2,0},{3,1},{4,6},{5,7},{6,4},{7,5},{8,10},{9,11},{10,... | collective-permute-start | bytes 1462280 | tf_op jit(solution)/shard_map/ppermute | solution.py:84
  62.3 64.7 %collective-permute-start.12 = (bf16[68,3584]{1,0:T(8,128)(2,1)}, bf16[68,3584]{1,0:T(8,128)(2,1)S(1)}, u32[]{:S(2)}, u32[]{:S(2)}) collective-permute-start(bf16[68,3584]{1,0:T(8,128)(2,1)} %get-tuple-element.81), channel_id=1, source_target_pairs={{0,2},{1,3},{2,0},{3,1},{4,6},{5,7},{6,4},{7,5},{8,10},{9,11},{10,... | collective-permute-start | bytes 1462280 | tf_op jit(solution)/shard_map/ppermute | solution.py:84
  63.2 65.0 %collective-permute-start.13 = (bf16[68,3584]{1,0:T(8,128)(2,1)}, bf16[68,3584]{1,0:T(8,128)(2,1)S(1)}, u32[]{:S(2)}, u32[]{:S(2)}) collective-permute-start(bf16[68,3584]{1,0:T(8,128)(2,1)} %get-tuple-element.80), channel_id=1, source_target_pairs={{0,4},{1,5},{2,6},{3,7},{4,0},{5,1},{6,2},{7,3},{8,12},{9,13},{10,... | collective-permute-start | bytes 1462280 | tf_op jit(solution)/shard_map/ppermute | solution.py:84
  124.9 81.2 %collective-permute-start.37 = (bf16[64,3584]{1,0:T(8,128)(2,1)}, bf16[64,3584]{1,0:T(8,128)(2,1)}, u32[]{:S(2)}, u32[]{:S(2)}) collective-permute-start(bf16[64,3584]{1,0:T(8,128)(2,1)} %get-tuple-element.97), channel_id=1, source_target_pairs={{0,1},{1,0},{2,3},{3,2},{4,5},{5,4},{6,7},{7,6},{8,9},{9,8},{10,11... | collective-permute-start | bytes 1376264 | tf_op jit(solution)/shard_map/ppermute | solution.py:84
  131.8 190.8 %collective-permute-start.28 = (bf16[128,1152]{1,0:T(8,128)(2,1)S(1)}, bf16[128,1152]{1,0:T(8,128)(2,1)}, u32[]{:S(2)}, u32[]{:S(2)}) collective-permute-start(bf16[128,1152]{1,0:T(8,128)(2,1)S(1)} %slice.172), channel_id=1, source_target_pairs={{0,8},{8,16},{16,24},{1,9},{9,17},{17,25},{2,10},{10,18},{18,26},{... | collective-permute-start | bytes 884744 | tf_op jit(solution)/shard_map/ppermute | solution.py:119
  137.4 31.3 %collective-permute-start.6 = (bf16[68,3584]{1,0:T(8,128)(2,1)}, bf16[68,3584]{1,0:T(8,128)(2,1)}, u32[]{:S(2)}, u32[]{:S(2)}) collective-permute-start(bf16[68,3584]{1,0:T(8,128)(2,1)} %get-tuple-element.90), channel_id=1, source_target_pairs={{0,2},{1,3},{2,0},{3,1},{4,6},{5,7},{6,4},{7,5},{8,10},{9,11},{10,... | collective-permute-start | bytes 1462280 | tf_op jit(solution)/shard_map/ppermute | solution.py:84
  137.4 38.1 %collective-permute-start.7 = (bf16[68,3584]{1,0:T(8,128)(2,1)}, bf16[68,3584]{1,0:T(8,128)(2,1)}, u32[]{:S(2)}, u32[]{:S(2)}) collective-permute-start(bf16[68,3584]{1,0:T(8,128)(2,1)} %get-tuple-element.89), channel_id=1, source_target_pairs={{0,4},{1,5},{2,6},{3,7},{4,0},{5,1},{6,2},{7,3},{8,12},{9,13},{10,... | collective-permute-start | bytes 1462280 | tf_op jit(solution)/shard_map/ppermute | solution.py:84
  140.5 35.1 %collective-permute-start.8 = (bf16[68,3584]{1,0:T(8,128)(2,1)}, bf16[68,3584]{1,0:T(8,128)(2,1)}, u32[]{:S(2)}, u32[]{:S(2)}) collective-permute-start(bf16[68,3584]{1,0:T(8,128)(2,1)} %get-tuple-element.88), channel_id=1, source_target_pairs={{0,6},{1,7},{2,4},{3,5},{4,2},{5,3},{6,0},{7,1},{8,14},{9,15},{10,... | collective-permute-start | bytes 1462280 | tf_op jit(solution)/shard_map/ppermute | solution.py:84
  175.6 30.7 %collective-permute-start.17 = (bf16[68,3584]{1,0:T(8,128)(2,1)}, bf16[68,3584]{1,0:T(8,128)(2,1)}, u32[]{:S(2)}, u32[]{:S(2)}) collective-permute-start(bf16[68,3584]{1,0:T(8,128)(2,1)} %get-tuple-element.79), channel_id=1, source_target_pairs={{0,6},{1,7},{2,4},{3,5},{4,2},{5,3},{6,0},{7,1},{8,14},{9,15},{10,... | collective-permute-start | bytes 1462280 | tf_op jit(solution)/shard_map/ppermute | solution.py:84
  177.9 54.4 %collective-permute-start.36 = (bf16[68,3584]{1,0:T(8,128)(2,1)}, bf16[68,3584]{1,0:T(8,128)(2,1)}, u32[]{:S(2)}, u32[]{:S(2)}) collective-permute-start(bf16[68,3584]{1,0:T(8,128)(2,1)} %get-tuple-element.77), channel_id=1, source_target_pairs={{0,4},{1,5},{2,6},{3,7},{4,0},{5,1},{6,2},{7,3},{8,12},{9,13},{10,... | collective-permute-start | bytes 1462280 | tf_op jit(solution)/shard_map/ppermute | solution.py:84
  198.9 33.4 %collective-permute-start.35 = (bf16[68,3584]{1,0:T(8,128)(2,1)}, bf16[68,3584]{1,0:T(8,128)(2,1)}, u32[]{:S(2)}, u32[]{:S(2)}) collective-permute-start(bf16[68,3584]{1,0:T(8,128)(2,1)} %get-tuple-element.78), channel_id=1, source_target_pairs={{0,2},{1,3},{2,0},{3,1},{4,6},{5,7},{6,4},{7,5},{8,10},{9,11},{10,... | collective-permute-start | bytes 1462280 | tf_op jit(solution)/shard_map/ppermute | solution.py:84
  206.1 57.4 %collective-permute-start.16 = (f32[272,1024]{1,0:T(8,128)S(1)}, f32[272,1024]{1,0:T(8,128)S(1)}, u32[]{:S(2)}, u32[]{:S(2)}) collective-permute-start(f32[272,1024]{1,0:T(8,128)S(1)} %fusion.10), channel_id=1, source_target_pairs={{0,1},{1,0},{2,3},{3,2},{4,5},{5,4},{6,7},{7,6},{8,9},{9,8},{10,11... | collective-permute-start | bytes 3342344 | tf_op jit(solution)/shard_map/ppermute | solution.py:84
  239.3 23.2 %collective-permute-start.40 = (bf16[64,3584]{1,0:T(8,128)(2,1)S(1)}, bf16[64,3584]{1,0:T(8,128)(2,1)S(1)}, u32[]{:S(2)}, u32[]{:S(2)}) collective-permute-start(bf16[64,3584]{1,0:T(8,128)(2,1)S(1)} %get-tuple-element.94), channel_id=1, source_target_pairs={{8,0},{9,1},{10,2},{11,3},{12,4},{13,5},{14,6},{15,7},{16,8},{17,9... | collective-permute-start | bytes 1376264 | tf_op jit(solution)/shard_map/ppermute | solution.py:131
  268.4 21.8 %collective-permute-start.24 = (bf16[68,1152]{1,0:T(8,128)(2,1)S(1)}, bf16[68,1152]{1,0:T(8,128)(2,1)S(1)}, u32[]{:S(2)}, u32[]{:S(2)}) collective-permute-start(bf16[68,1152]{1,0:T(8,128)(2,1)S(1)} %get-tuple-element.114), channel_id=1, source_target_pairs={{0,4},{1,5},{2,6},{3,7},{4,0},{5,1},{6,2},{7,3},{8,12},{9,13},{10,... | collective-permute-start | bytes 470024 | tf_op jit(solution)/shard_map/ppermute | solution.py:84
  268.4 21.8 %collective-permute-start.23 = (bf16[68,1152]{1,0:T(8,128)(2,1)S(1)}, bf16[68,1152]{1,0:T(8,128)(2,1)S(1)}, u32[]{:S(2)}, u32[]{:S(2)}) collective-permute-start(bf16[68,1152]{1,0:T(8,128)(2,1)S(1)} %get-tuple-element.115), channel_id=1, source_target_pairs={{0,2},{1,3},{2,0},{3,1},{4,6},{5,7},{6,4},{7,5},{8,10},{9,11},{10,... | collective-permute-start | bytes 470024 | tf_op jit(solution)/shard_map/ppermute | solution.py:84
  271.3 23.3 %collective-permute-start.20 = (bf16[68,1280]{1,0:T(8,128)(2,1)S(1)}, bf16[68,1280]{1,0:T(8,128)(2,1)S(1)}, u32[]{:S(2)}, u32[]{:S(2)}) collective-permute-start(bf16[68,1280]{1,0:T(8,128)(2,1)S(1)} %get-tuple-element.105), channel_id=1, source_target_pairs={{0,6},{1,7},{2,4},{3,5},{4,2},{5,3},{6,0},{7,1},{8,14},{9,15},{10,... | collective-permute-start | bytes 522248 | tf_op jit(solution)/shard_map/ppermute | solution.py:84
  275.0 22.5 %collective-permute-start.19 = (bf16[68,1280]{1,0:T(8,128)(2,1)S(1)}, bf16[68,1280]{1,0:T(8,128)(2,1)S(1)}, u32[]{:S(2)}, u32[]{:S(2)}) collective-permute-start(bf16[68,1280]{1,0:T(8,128)(2,1)S(1)} %get-tuple-element.106), channel_id=1, source_target_pairs={{0,4},{1,5},{2,6},{3,7},{4,0},{5,1},{6,2},{7,3},{8,12},{9,13},{10,... | collective-permute-start | bytes 522248 | tf_op jit(solution)/shard_map/ppermute | solution.py:84
  290.1 15.4 %collective-permute-start.30 = (bf16[272,1152]{1,0:T(8,128)(2,1)S(1)}, bf16[272,1152]{1,0:T(8,128)(2,1)S(1)}, u32[]{:S(2)}, u32[]{:S(2)}) collective-permute-start(bf16[272,1152]{1,0:T(8,128)(2,1)S(1)} %convolution_convert_fusion.4), channel_id=1, source_target_pairs={{0,8},{8,16},{16,24},{1,9},{9,17},{17,25},{2,10},{10,18},{18,26},{... | collective-permute-start | bytes 1880072 | tf_op jit(solution)/shard_map/ppermute | solution.py:119
  294.6 29.4 %collective-permute-start.26 = (bf16[64,1152]{1,0:T(8,128)(2,1)S(1)}, bf16[64,1152]{1,0:T(8,128)(2,1)S(1)}, u32[]{:S(2)}, u32[]{:S(2)}) collective-permute-start(bf16[64,1152]{1,0:T(8,128)(2,1)S(1)} %get-tuple-element.119), channel_id=1, source_target_pairs={{0,9},{1,8},{2,11},{3,10},{4,13},{5,12},{6,15},{7,14},{8,17},{9,16... | collective-permute-start | bytes 442376 | tf_op jit(solution)/shard_map/ppermute | solution.py:131
  (44 other events, 582.5 us)

commit v4 on v3

--- a/solution.py
+++ b/solution.py
@@ -266,8 +266,9 @@
     for c, (x_c, gates_c, hots_c) in enumerate(sources):
         done_a = jnp.concatenate(chunks[c], axis=0)
         mixed = x_c.astype(jnp.float32)
-        for j, h in enumerate(hots_c):
-            mixed = mixed + gates_c[:, j : j + 1] * dot(h, done_a)
+        taken = jnp.split(dot(jnp.concatenate(hots_c, axis=0), done_a), top, axis=0)
+        for j, rows in enumerate(taken):
+            mixed = mixed + gates_c[:, j : j + 1] * rows
         mixed = mixed.astype(jnp.bfloat16)
         if c < CHUNKS - 1:
             passed.append(pass_on(mixed, 1))

time: 327 us -> 325 us (level)
  matrix products: 48.5 us -> 44.3 us
    dot_general x22 -> x19, matrix products: 48.5 us -> 44.3 us  [dot(): return lax.dot_general(a, b, dims, preferred_element_type=jnp.float32)]
where the time goes in v4:
time: 325 us
  starting transfers between devices  111 us (34%)
  waiting for transfers between devices  105 us (32%)
  other arithmetic  51.4 us (16%)
  matrix products  44.3 us (14%)
  local copies, waits for them, and re-layouts  8.8 us (3%)
  between operations  4.25 us (1%)
    ppermute x35, waiting for transfers between devices, swap(): lax.ppermute(value, 'expert', [(i, i ^ distance) for i in range(peers)])  87.3 us
    ppermute x35, starting transfers between devices, swap(): lax.ppermute(value, 'expert', [(i, i ^ distance) for i in range(peers)])  86 us
    dot_general x19, matrix products, dot(): return lax.dot_general(a, b, dims, preferred_element_type=jnp.float32)  44.3 us
    convert_element_type x2, other arithmetic, fake_quant(): t.astype(jnp.bfloat16)  36.6 us
    ppermute x6, waiting for transfers between devices, pass_on(): pieces.append(lax.ppermute(block, ('pipe', 'expert'), pairs))  18 us
    ppermute x6, starting transfers between devices, pass_on(): pieces.append(lax.ppermute(block, ('pipe', 'expert'), pairs))  13.2 us
    ppermute x3, starting transfers between devices, ahead(): return lax.ppermute(value, 'pipe', [(s, s + 1) for s in range(stages - 1)])  11.3 us
  transfers between devices with their start and end apart: 44, of which 19 were waited for; matrix products, arithmetic and copies ran while one was open for 24% of the time, Pallas kernels for 0%

profile of v4, /device:TPU:0, one launch (start us, length us, event | category | flops | bytes accessed | tf_op | source)
XLA Modules:
  0.0 324.7 jit_solution(2070012844245811293)
XLA Ops:
  13.9 18.3 %subtract_convert_fusion.1 = (bf16[3584,1024]{1,0:T(8,128)(2,1)S(1)}, bf16[3584,1024]{1,0:T(8,128)(2,1)}, bf16[3584,1024]{1,0:T(8,128)(2,1)S(1)}) fusion(bf16[3584,1024]{1,0:T(8,128)(2,1)S(1)} %bitcast.131, f32[]{:T(128)S(6)} %div.66, f32[]{:T(128)} %fusion.116), kind=kLoop, calls=%fused_computation.8 | loop fusion | flops 128450560 | bytes 29360136 | tf_op jit(solution)/shard_map/convert_element_type | solution.py:37
  32.8 4.7 %collective-permute-start.5 = (bf16[68,3584]{1,0:T(8,128)(2,1)S(1)}, bf16[68,3584]{1,0:T(8,128)(2,1)S(1)}, u32[]{:S(2)}, u32[]{:S(2)}) collective-permute-start(bf16[68,3584]{1,0:T(8,128)(2,1)S(1)} %get-tuple-element.83), channel_id=1, source_target_pairs={{0,6},{1,7},{2,4},{3,5},{4,2},{5,3},{6,0},{7,1},{8,14},{9,15},{10,... | collective-permute-start | bytes 1462280 | tf_op jit(solution)/shard_map/ppermute | solution.py:84
  38.5 18.3 %subtract_convert_fusion = (bf16[1024,3584]{1,0:T(8,128)(2,1)}, bf16[1024,3584]{1,0:T(8,128)(2,1)}, bf16[1024,3584]{1,0:T(8,128)(2,1)S(1)}) fusion(bf16[1024,3584]{1,0:T(8,128)(2,1)S(1)} %bitcast.134, f32[]{:T(128)S(6)} %div.68, f32[]{:T(128)} %fusion.117), kind=kLoop, calls=%fused_computation.6 | loop fusion | flops 128450560 | bytes 29360136 | tf_op jit(solution)/shard_map/convert_element_type | solution.py:37
  57.9 3.4 %collective-permute-start.9 = (bf16[68,3584]{1,0:T(8,128)(2,1)S(1)}, bf16[68,3584]{1,0:T(8,128)(2,1)S(1)}, u32[]{:S(2)}, u32[]{:S(2)}) collective-permute-start(bf16[68,3584]{1,0:T(8,128)(2,1)S(1)} %get-tuple-element.87), channel_id=1, source_target_pairs={{0,2},{1,3},{2,0},{3,1},{4,6},{5,7},{6,4},{7,5},{8,10},{9,11},{10,... | collective-permute-start | bytes 1462280 | tf_op jit(solution)/shard_map/ppermute | solution.py:84
  63.9 31.5 %collective-permute-start.13 = (bf16[68,3584]{1,0:T(8,128)(2,1)S(1)}, bf16[68,3584]{1,0:T(8,128)(2,1)S(1)}, u32[]{:S(2)}, u32[]{:S(2)}) collective-permute-start(bf16[68,3584]{1,0:T(8,128)(2,1)S(1)} %get-tuple-element.80), channel_id=1, source_target_pairs={{0,4},{1,5},{2,6},{3,7},{4,0},{5,1},{6,2},{7,3},{8,12},{9,13},{10,... | collective-permute-start | bytes 1462280 | tf_op jit(solution)/shard_map/ppermute | solution.py:84
  95.3 20.5 %collective-permute-done.10 = bf16[68,3584]{1,0:T(8,128)(2,1)S(1)} collective-permute-done((bf16[68,3584]{1,0:T(8,128)(2,1)}, bf16[68,3584]{1,0:T(8,128)(2,1)S(1)}, u32[]{:S(2)}, u32[]{:S(2)}) %collective-permute-start.10) | collective-permute-done | bytes 487456 | tf_op jit(solution)/shard_map/ppermute | solution.py:84
  115.9 3.6 %collective-permute-start.29 = (f32[128,4]{0,1:T(4,128)S(1)}, f32[128,4]{0,1:T(4,128)S(1)}, u32[]{:S(2)}, u32[]{:S(2)}) collective-permute-start(f32[128,4]{0,1:T(4,128)S(1)} %concatenate.88), channel_id=1, source_target_pairs={{0,8},{8,16},{16,24},{1,9},{9,17},{17,25},{2,10},{10,18},{18,26},{... | collective-permute-start | bytes 6152 | tf_op jit(solution)/shard_map/ppermute | solution.py:119
  130.4 4.1 %collective-permute-start.28 = (bf16[128,1152]{1,0:T(8,128)(2,1)}, bf16[128,1152]{1,0:T(8,128)(2,1)}, u32[]{:S(2)}, u32[]{:S(2)}) collective-permute-start(bf16[128,1152]{1,0:T(8,128)(2,1)} %slice.172), channel_id=1, source_target_pairs={{0,8},{8,16},{16,24},{1,9},{9,17},{17,25},{2,10},{10,18},{18,26},{... | collective-permute-start | bytes 884744 | tf_op jit(solution)/shard_map/ppermute | solution.py:119
  143.0 11.1 %multiply_reduce_fusion.1 = (f32[]{:T(128)}, bf16[3584,1024]{1,0:T(8,128)(2,1)}) fusion(bf16[3584,1024]{1,0:T(8,128)(2,1)S(1)} %get-tuple-element.58, bf16[3584,1024]{1,0:T(8,128)(2,1)} %get-tuple-element.49, bf16[272,3584]{1,0:T(8,128)(2,1)} %copy-done.4, bf16[272,1024]{1,0:T(8,128)(2,1)S(1)} %multiply_convert_fusion.7), kind=kOutput, calls=%fused_computation.3 | convolution fusion | flops 2018508800 | bytes 24526852 | tf_op jit(solution)/shard_map/dot_general | solution.py:46
  154.2 11.6 %multiply_reduce_fusion = (f32[]{:T(128)}, bf16[1024,3584]{1,0:T(8,128)(2,1)}) fusion(bf16[1024,3584]{1,0:T(8,128)(2,1)} %get-tuple-element.59, bf16[1024,3584]{1,0:T(8,128)(2,1)} %get-tuple-element.51, bf16[272,3584]{1,0:T(8,128)(2,1)S(1)} %copy-done.6, f32[272,1024]{1,0:T(8,128)S(1)} %add_reduce-precision_fusion), kind=kOutput, calls=%fused_computation.2 | convolution fusion | flops 2019901440 | bytes 25083908 | tf_op jit(solution)/shard_map/dot_general | solution.py:46
  167.2 6.8 %collective-permute-done.7 = bf16[68,3584]{1,0:T(8,128)(2,1)} collective-permute-done((bf16[68,3584]{1,0:T(8,128)(2,1)}, bf16[68,3584]{1,0:T(8,128)(2,1)}, u32[]{:S(2)}, u32[]{:S(2)}) %collective-permute-start.7) | collective-permute-done | bytes 487456 | tf_op jit(solution)/shard_map/ppermute | solution.py:84
  176.3 21.0 %collective-permute-start.36 = (bf16[68,3584]{1,0:T(8,128)(2,1)}, bf16[68,3584]{1,0:T(8,128)(2,1)S(1)}, u32[]{:S(2)}, u32[]{:S(2)}) collective-permute-start(bf16[68,3584]{1,0:T(8,128)(2,1)} %get-tuple-element.77), channel_id=1, source_target_pairs={{0,4},{1,5},{2,6},{3,7},{4,0},{5,1},{6,2},{7,3},{8,12},{9,13},{10,... | collective-permute-start | bytes 1462280 | tf_op jit(solution)/shard_map/ppermute | solution.py:84
  198.7 6.0 %fusion.10 = f32[272,1024]{1,0:T(8,128)S(1)} fusion(bf16[3584,1024]{1,0:T(8,128)(2,1)} %copy-done.2, bf16[68,3584]{1,0:T(8,128)(2,1)} %collective-permute-done.8, bf16[68,3584]{1,0:T(8,128)(2,1)} %collective-permute-done.7, bf16[68,3584]{1,0:T(8,128)(2,1)} %collective-permute-done.6, bf16[68,3584]{1,0:T(8,128)(2,1)} %get-tuple-element.52), kind=kOutput, calls=%fused_computation.45 | convolution fusion | flops 2004287488 | bytes 10403840 | tf_op jit(solution)/shard_map/dot_general | solution.py:46
  204.8 25.9 %collective-permute-done.36 = bf16[68,3584]{1,0:T(8,128)(2,1)S(1)} collective-permute-done((bf16[68,3584]{1,0:T(8,128)(2,1)}, bf16[68,3584]{1,0:T(8,128)(2,1)S(1)}, u32[]{:S(2)}, u32[]{:S(2)}) %collective-permute-start.36) | collective-permute-done | bytes 487456 | tf_op jit(solution)/shard_map/ppermute | solution.py:84
  238.8 3.6 %collective-permute-done.42 = f32[2,4]{1,0:T(2,128)S(1)} collective-permute-done((f32[2,4]{1,0:T(2,128)S(1)}, f32[2,4]{1,0:T(2,128)S(1)}, u32[]{:S(2)}, u32[]{:S(2)}) %collective-permute-start.42) | collective-permute-done | bytes 64 | tf_op jit(solution)/shard_map/ppermute | solution.py:84
  243.3 3.6 %collective-permute-done.43 = f32[2,4]{1,0:T(2,128)S(1)} collective-permute-done((f32[2,4]{1,0:T(2,128)S(1)}, f32[2,4]{1,0:T(2,128)S(1)}, u32[]{:S(2)}, u32[]{:S(2)}) %collective-permute-start.43) | collective-permute-done | bytes 64 | tf_op jit(solution)/shard_map/ppermute | solution.py:84
  250.2 10.2 %collective-permute-done.40 = bf16[64,3584]{1,0:T(8,128)(2,1)S(1)} collective-permute-done((bf16[64,3584]{1,0:T(8,128)(2,1)S(1)}, bf16[64,3584]{1,0:T(8,128)(2,1)S(1)}, u32[]{:S(2)}, u32[]{:S(2)}) %collective-permute-start.40) | collective-permute-done | bytes 458784 | tf_op jit(solution)/shard_map/ppermute | solution.py:131
  272.9 3.3 %collective-permute-start.19 = (bf16[68,1280]{1,0:T(8,128)(2,1)S(1)}, bf16[68,1280]{1,0:T(8,128)(2,1)S(1)}, u32[]{:S(2)}, u32[]{:S(2)}) collective-permute-start(bf16[68,1280]{1,0:T(8,128)(2,1)S(1)} %get-tuple-element.106), channel_id=1, source_target_pairs={{0,4},{1,5},{2,6},{3,7},{4,0},{5,1},{6,2},{7,3},{8,12},{9,13},{10,... | collective-permute-start | bytes 522248 | tf_op jit(solution)/shard_map/ppermute | solution.py:84
  276.2 12.1 %collective-permute-done.24 = bf16[68,1152]{1,0:T(8,128)(2,1)S(1)} collective-permute-done((bf16[68,1152]{1,0:T(8,128)(2,1)S(1)}, bf16[68,1152]{1,0:T(8,128)(2,1)S(1)}, u32[]{:S(2)}, u32[]{:S(2)}) %collective-permute-start.24) | collective-permute-done | bytes 156704 | tf_op jit(solution)/shard_map/ppermute | solution.py:84
  288.2 3.6 %collective-permute-start.30 = (bf16[272,1152]{1,0:T(8,128)(2,1)S(1)}, bf16[272,1152]{1,0:T(8,128)(2,1)S(1)}, u32[]{:S(2)}, u32[]{:S(2)}) collective-permute-start(bf16[272,1152]{1,0:T(8,128)(2,1)S(1)} %convolution_convert_fusion.4), channel_id=1, source_target_pairs={{0,8},{8,16},{16,24},{1,9},{9,17},{17,25},{2,10},{10,18},{18,26},{... | collective-permute-start | bytes 1880072 | tf_op jit(solution)/shard_map/ppermute | solution.py:119
  299.2 4.2 %collective-permute-start.22 = (bf16[64,1280]{1,0:T(8,128)(2,1)S(1)}, bf16[64,1280]{1,0:T(8,128)(2,1)S(1)}, u32[]{:S(2)}, u32[]{:S(2)}) collective-permute-start(bf16[64,1280]{1,0:T(8,128)(2,1)S(1)} %get-tuple-element.116), channel_id=1, source_target_pairs={{0,8},{1,9},{2,10},{3,11},{4,12},{5,13},{6,14},{7,15},{8,16},{9,17... | collective-permute-start | bytes 491528 | tf_op jit(solution)/shard_map/ppermute | solution.py:131
  303.6 3.3 %collective-permute-done.21 = bf16[64,1280]{1,0:T(8,128)(2,1)S(1)} collective-permute-done((bf16[64,1280]{1,0:T(8,128)(2,1)S(1)}, bf16[64,1280]{1,0:T(8,128)(2,1)S(1)}, u32[]{:S(2)}, u32[]{:S(2)}) %collective-permute-start.21) | collective-permute-done | bytes 163872 | tf_op jit(solution)/shard_map/ppermute | solution.py:131
  312.6 3.6 %collective-permute-start.27 = (bf16[64,1152]{1,0:T(8,128)(2,1)S(1)}, bf16[64,1152]{1,0:T(8,128)(2,1)S(1)}, u32[]{:S(2)}, u32[]{:S(2)}) collective-permute-start(bf16[64,1152]{1,0:T(8,128)(2,1)S(1)} %get-tuple-element.118), channel_id=1, source_target_pairs={{0,8},{1,9},{2,10},{3,11},{4,12},{5,13},{6,14},{7,15},{8,16},{9,17... | collective-permute-start | bytes 442376 | tf_op jit(solution)/shard_map/ppermute | solution.py:131
  316.2 4.2 %collective-permute-done.32 = bf16[68,1152]{1,0:T(8,128)(2,1)S(1)} collective-permute-done((bf16[68,1152]{1,0:T(8,128)(2,1)S(1)}, bf16[68,1152]{1,0:T(8,128)(2,1)S(1)}, u32[]{:S(2)}, u32[]{:S(2)}) %collective-permute-start.32) | collective-permute-done | bytes 156704 | tf_op jit(solution)/shard_map/ppermute | solution.py:84
  (218 shorter events, 82.1 us)
Async XLA Ops:
  32.2 30.2 %collective-permute-start.3 = (bf16[64,3584]{1,0:T(8,128)(2,1)S(1)}, bf16[64,3584]{1,0:T(8,128)(2,1)S(1)}, u32[]{:S(2)}, u32[]{:S(2)}) collective-permute-start(bf16[64,3584]{1,0:T(8,128)(2,1)S(1)} %get-tuple-element.99), channel_id=1, source_target_pairs={{0,1},{1,0},{2,3},{3,2},{4,5},{5,4},{6,7},{7,6},{8,9},{9,8},{10,11... | collective-permute-start | bytes 1376264 | tf_op jit(solution)/shard_map/ppermute | solution.py:84
  32.3 25.6 %collective-permute-start.4 = (f32[64,6]{0,1:T(8,128)S(1)}, f32[64,6]{0,1:T(8,128)S(1)}, u32[]{:S(2)}, u32[]{:S(2)}) collective-permute-start(f32[64,6]{0,1:T(8,128)S(1)} %pad_maximum_fusion.8), channel_id=1, source_target_pairs={{0,1},{1,0},{2,3},{3,2},{4,5},{5,4},{6,7},{7,6},{8,9},{9,8},{10,11... | collective-permute-start | bytes 4616 | tf_op jit(solution)/shard_map/ppermute | solution.py:84
  32.8 92.3 %collective-permute-start.5 = (bf16[68,3584]{1,0:T(8,128)(2,1)S(1)}, bf16[68,3584]{1,0:T(8,128)(2,1)S(1)}, u32[]{:S(2)}, u32[]{:S(2)}) collective-permute-start(bf16[68,3584]{1,0:T(8,128)(2,1)S(1)} %get-tuple-element.83), channel_id=1, source_target_pairs={{0,6},{1,7},{2,4},{3,5},{4,2},{5,3},{6,0},{7,1},{8,14},{9,15},{10,... | collective-permute-start | bytes 1462280 | tf_op jit(solution)/shard_map/ppermute | solution.py:84
  37.5 26.4 %collective-permute-start.11 = (bf16[68,3584]{1,0:T(8,128)(2,1)}, bf16[68,3584]{1,0:T(8,128)(2,1)S(1)}, u32[]{:S(2)}, u32[]{:S(2)}) collective-permute-start(bf16[68,3584]{1,0:T(8,128)(2,1)} %get-tuple-element.85), channel_id=1, source_target_pairs={{0,6},{1,7},{2,4},{3,5},{4,2},{5,3},{6,0},{7,1},{8,14},{9,15},{10,... | collective-permute-start | bytes 1462280 | tf_op jit(solution)/shard_map/ppermute | solution.py:84
  37.6 78.3 %collective-permute-start.10 = (bf16[68,3584]{1,0:T(8,128)(2,1)}, bf16[68,3584]{1,0:T(8,128)(2,1)S(1)}, u32[]{:S(2)}, u32[]{:S(2)}) collective-permute-start(bf16[68,3584]{1,0:T(8,128)(2,1)} %get-tuple-element.86), channel_id=1, source_target_pairs={{0,4},{1,5},{2,6},{3,7},{4,0},{5,1},{6,2},{7,3},{8,12},{9,13},{10,... | collective-permute-start | bytes 1462280 | tf_op jit(solution)/shard_map/ppermute | solution.py:84
  57.9 57.9 %collective-permute-start.9 = (bf16[68,3584]{1,0:T(8,128)(2,1)S(1)}, bf16[68,3584]{1,0:T(8,128)(2,1)S(1)}, u32[]{:S(2)}, u32[]{:S(2)}) collective-permute-start(bf16[68,3584]{1,0:T(8,128)(2,1)S(1)} %get-tuple-element.87), channel_id=1, source_target_pairs={{0,2},{1,3},{2,0},{3,1},{4,6},{5,7},{6,4},{7,5},{8,10},{9,11},{10,... | collective-permute-start | bytes 1462280 | tf_op jit(solution)/shard_map/ppermute | solution.py:84
  62.4 62.7 %collective-permute-start.12 = (bf16[68,3584]{1,0:T(8,128)(2,1)S(1)}, bf16[68,3584]{1,0:T(8,128)(2,1)S(1)}, u32[]{:S(2)}, u32[]{:S(2)}) collective-permute-start(bf16[68,3584]{1,0:T(8,128)(2,1)S(1)} %get-tuple-element.81), channel_id=1, source_target_pairs={{0,2},{1,3},{2,0},{3,1},{4,6},{5,7},{6,4},{7,5},{8,10},{9,11},{10,... | collective-permute-start | bytes 1462280 | tf_op jit(solution)/shard_map/ppermute | solution.py:84
  63.9 62.5 %collective-permute-start.13 = (bf16[68,3584]{1,0:T(8,128)(2,1)S(1)}, bf16[68,3584]{1,0:T(8,128)(2,1)S(1)}, u32[]{:S(2)}, u32[]{:S(2)}) collective-permute-start(bf16[68,3584]{1,0:T(8,128)(2,1)S(1)} %get-tuple-element.80), channel_id=1, source_target_pairs={{0,4},{1,5},{2,6},{3,7},{4,0},{5,1},{6,2},{7,3},{8,12},{9,13},{10,... | collective-permute-start | bytes 1462280 | tf_op jit(solution)/shard_map/ppermute | solution.py:84
  115.9 88.8 %collective-permute-start.37 = (bf16[64,3584]{1,0:T(8,128)(2,1)}, bf16[64,3584]{1,0:T(8,128)(2,1)}, u32[]{:S(2)}, u32[]{:S(2)}) collective-permute-start(bf16[64,3584]{1,0:T(8,128)(2,1)} %get-tuple-element.97), channel_id=1, source_target_pairs={{0,1},{1,0},{2,3},{3,2},{4,5},{5,4},{6,7},{7,6},{8,9},{9,8},{10,11... | collective-permute-start | bytes 1376264 | tf_op jit(solution)/shard_map/ppermute | solution.py:84
  130.4 190.5 %collective-permute-start.28 = (bf16[128,1152]{1,0:T(8,128)(2,1)}, bf16[128,1152]{1,0:T(8,128)(2,1)}, u32[]{:S(2)}, u32[]{:S(2)}) collective-permute-start(bf16[128,1152]{1,0:T(8,128)(2,1)} %slice.172), channel_id=1, source_target_pairs={{0,8},{8,16},{16,24},{1,9},{9,17},{17,25},{2,10},{10,18},{18,26},{... | collective-permute-start | bytes 884744 | tf_op jit(solution)/shard_map/ppermute | solution.py:119
  135.9 31.3 %collective-permute-start.6 = (bf16[68,3584]{1,0:T(8,128)(2,1)}, bf16[68,3584]{1,0:T(8,128)(2,1)}, u32[]{:S(2)}, u32[]{:S(2)}) collective-permute-start(bf16[68,3584]{1,0:T(8,128)(2,1)} %get-tuple-element.90), channel_id=1, source_target_pairs={{0,2},{1,3},{2,0},{3,1},{4,6},{5,7},{6,4},{7,5},{8,10},{9,11},{10,... | collective-permute-start | bytes 1462280 | tf_op jit(solution)/shard_map/ppermute | solution.py:84
  135.9 38.1 %collective-permute-start.7 = (bf16[68,3584]{1,0:T(8,128)(2,1)}, bf16[68,3584]{1,0:T(8,128)(2,1)}, u32[]{:S(2)}, u32[]{:S(2)}) collective-permute-start(bf16[68,3584]{1,0:T(8,128)(2,1)} %get-tuple-element.89), channel_id=1, source_target_pairs={{0,4},{1,5},{2,6},{3,7},{4,0},{5,1},{6,2},{7,3},{8,12},{9,13},{10,... | collective-permute-start | bytes 1462280 | tf_op jit(solution)/shard_map/ppermute | solution.py:84
  138.9 35.1 %collective-permute-start.8 = (bf16[68,3584]{1,0:T(8,128)(2,1)}, bf16[68,3584]{1,0:T(8,128)(2,1)}, u32[]{:S(2)}, u32[]{:S(2)}) collective-permute-start(bf16[68,3584]{1,0:T(8,128)(2,1)} %get-tuple-element.88), channel_id=1, source_target_pairs={{0,6},{1,7},{2,4},{3,5},{4,2},{5,3},{6,0},{7,1},{8,14},{9,15},{10,... | collective-permute-start | bytes 1462280 | tf_op jit(solution)/shard_map/ppermute | solution.py:84
  174.0 30.8 %collective-permute-start.17 = (bf16[68,3584]{1,0:T(8,128)(2,1)}, bf16[68,3584]{1,0:T(8,128)(2,1)S(1)}, u32[]{:S(2)}, u32[]{:S(2)}) collective-permute-start(bf16[68,3584]{1,0:T(8,128)(2,1)} %get-tuple-element.79), channel_id=1, source_target_pairs={{0,6},{1,7},{2,4},{3,5},{4,2},{5,3},{6,0},{7,1},{8,14},{9,15},{10,... | collective-permute-start | bytes 1462280 | tf_op jit(solution)/shard_map/ppermute | solution.py:84
  176.3 54.3 %collective-permute-start.36 = (bf16[68,3584]{1,0:T(8,128)(2,1)}, bf16[68,3584]{1,0:T(8,128)(2,1)S(1)}, u32[]{:S(2)}, u32[]{:S(2)}) collective-permute-start(bf16[68,3584]{1,0:T(8,128)(2,1)} %get-tuple-element.77), channel_id=1, source_target_pairs={{0,4},{1,5},{2,6},{3,7},{4,0},{5,1},{6,2},{7,3},{8,12},{9,13},{10,... | collective-permute-start | bytes 1462280 | tf_op jit(solution)/shard_map/ppermute | solution.py:84
  197.4 33.3 %collective-permute-start.35 = (bf16[68,3584]{1,0:T(8,128)(2,1)}, bf16[68,3584]{1,0:T(8,128)(2,1)S(1)}, u32[]{:S(2)}, u32[]{:S(2)}) collective-permute-start(bf16[68,3584]{1,0:T(8,128)(2,1)} %get-tuple-element.78), channel_id=1, source_target_pairs={{0,2},{1,3},{2,0},{3,1},{4,6},{5,7},{6,4},{7,5},{8,10},{9,11},{10,... | collective-permute-start | bytes 1462280 | tf_op jit(solution)/shard_map/ppermute | solution.py:84
  204.7 56.7 %collective-permute-start.16 = (f32[272,1024]{1,0:T(8,128)S(1)}, f32[272,1024]{1,0:T(8,128)S(1)}, u32[]{:S(2)}, u32[]{:S(2)}) collective-permute-start(f32[272,1024]{1,0:T(8,128)S(1)} %fusion.10), channel_id=1, source_target_pairs={{0,1},{1,0},{2,3},{3,2},{4,5},{5,4},{6,7},{7,6},{8,9},{9,8},{10,11... | collective-permute-start | bytes 3342344 | tf_op jit(solution)/shard_map/ppermute | solution.py:84
  237.1 23.2 %collective-permute-start.40 = (bf16[64,3584]{1,0:T(8,128)(2,1)S(1)}, bf16[64,3584]{1,0:T(8,128)(2,1)S(1)}, u32[]{:S(2)}, u32[]{:S(2)}) collective-permute-start(bf16[64,3584]{1,0:T(8,128)(2,1)S(1)} %get-tuple-element.94), channel_id=1, source_target_pairs={{8,0},{9,1},{10,2},{11,3},{12,4},{13,5},{14,6},{15,7},{16,8},{17,9... | collective-permute-start | bytes 1376264 | tf_op jit(solution)/shard_map/ppermute | solution.py:131
  266.2 22.0 %collective-permute-start.24 = (bf16[68,1152]{1,0:T(8,128)(2,1)S(1)}, bf16[68,1152]{1,0:T(8,128)(2,1)S(1)}, u32[]{:S(2)}, u32[]{:S(2)}) collective-permute-start(bf16[68,1152]{1,0:T(8,128)(2,1)S(1)} %get-tuple-element.114), channel_id=1, source_target_pairs={{0,4},{1,5},{2,6},{3,7},{4,0},{5,1},{6,2},{7,3},{8,12},{9,13},{10,... | collective-permute-start | bytes 470024 | tf_op jit(solution)/shard_map/ppermute | solution.py:84
  266.2 22.0 %collective-permute-start.23 = (bf16[68,1152]{1,0:T(8,128)(2,1)S(1)}, bf16[68,1152]{1,0:T(8,128)(2,1)S(1)}, u32[]{:S(2)}, u32[]{:S(2)}) collective-permute-start(bf16[68,1152]{1,0:T(8,128)(2,1)S(1)} %get-tuple-element.115), channel_id=1, source_target_pairs={{0,2},{1,3},{2,0},{3,1},{4,6},{5,7},{6,4},{7,5},{8,10},{9,11},{10,... | collective-permute-start | bytes 470024 | tf_op jit(solution)/shard_map/ppermute | solution.py:84
  269.2 23.4 %collective-permute-start.20 = (bf16[68,1280]{1,0:T(8,128)(2,1)S(1)}, bf16[68,1280]{1,0:T(8,128)(2,1)S(1)}, u32[]{:S(2)}, u32[]{:S(2)}) collective-permute-start(bf16[68,1280]{1,0:T(8,128)(2,1)S(1)} %get-tuple-element.105), channel_id=1, source_target_pairs={{0,6},{1,7},{2,4},{3,5},{4,2},{5,3},{6,0},{7,1},{8,14},{9,15},{10,... | collective-permute-start | bytes 522248 | tf_op jit(solution)/shard_map/ppermute | solution.py:84
  272.9 22.6 %collective-permute-start.19 = (bf16[68,1280]{1,0:T(8,128)(2,1)S(1)}, bf16[68,1280]{1,0:T(8,128)(2,1)S(1)}, u32[]{:S(2)}, u32[]{:S(2)}) collective-permute-start(bf16[68,1280]{1,0:T(8,128)(2,1)S(1)} %get-tuple-element.106), channel_id=1, source_target_pairs={{0,4},{1,5},{2,6},{3,7},{4,0},{5,1},{6,2},{7,3},{8,12},{9,13},{10,... | collective-permute-start | bytes 522248 | tf_op jit(solution)/shard_map/ppermute | solution.py:84
  288.2 15.2 %collective-permute-start.30 = (bf16[272,1152]{1,0:T(8,128)(2,1)S(1)}, bf16[272,1152]{1,0:T(8,128)(2,1)S(1)}, u32[]{:S(2)}, u32[]{:S(2)}) collective-permute-start(bf16[272,1152]{1,0:T(8,128)(2,1)S(1)} %convolution_convert_fusion.4), channel_id=1, source_target_pairs={{0,8},{8,16},{16,24},{1,9},{9,17},{17,25},{2,10},{10,18},{18,26},{... | collective-permute-start | bytes 1880072 | tf_op jit(solution)/shard_map/ppermute | solution.py:119
  292.6 29.6 %collective-permute-start.26 = (bf16[64,1152]{1,0:T(8,128)(2,1)S(1)}, bf16[64,1152]{1,0:T(8,128)(2,1)S(1)}, u32[]{:S(2)}, u32[]{:S(2)}) collective-permute-start(bf16[64,1152]{1,0:T(8,128)(2,1)S(1)} %get-tuple-element.119), channel_id=1, source_target_pairs={{0,9},{1,8},{2,11},{3,10},{4,13},{5,12},{6,15},{7,14},{8,17},{9,16... | collective-permute-start | bytes 442376 | tf_op jit(solution)/shard_map/ppermute | solution.py:131
  (46 other events, 653.3 us)
